TPU v7x, 128 devices: a whole 4x4x4 slice. The times are simulated.
128 devices in a mesh: gx: 16 (over y, z_lo, core), gy: 8 (over x, z_hi).
Axes of the slice: x: 4, y: 4, z: 4 (z_hi: 2, z_lo: 2; z = z_hi * 2 + z_lo), core: 2. Of those that a mesh axis runs over, the one named last changes fastest.
Arguments:
- fields: bfloat16 [8, 256, 128, 128], P(None, ('gx', 'gy')), may hold values from -6 to 6
- w_lift: bfloat16 [3, 3, 3, 8, 64], replicated, may hold values from -0.4375 to 0.4375
- b_lift: float32 [64], replicated, may hold values from -3 to 3
- down_weight: bfloat16 [4, 4, 4, 64, 64], replicated, may hold values from -0.09375 to 0.09375
- b_down: float32 [64], replicated, may hold values from -3 to 3
- perf_well: int32 [128, 256], P(('gx', 'gy')), may hold values from -1 to 2047, as said below
- perf_cell: int32 [128, 256], P(('gx', 'gy')), may hold values from 0 to 4095, as said below
- perf_weight: float32 [128, 256], P(('gx', 'gy')), may hold values from 0.25 to 2
- well_slot: int32 [2048], replicated, may hold values from 0 to 2047, each once
- well_grad: bfloat16 [2048, 64], P(('gx', 'gy')), may hold values from -24 to 24
- field_grad: bfloat16 [64, 64, 64, 128], P(None, 'gx', 'gy'), may hold values from -6 to 6
Outputs:
- coarse: bfloat16 [64, 64, 64, 128], P(None, 'gx', 'gy')
- well_feat: float32 [2048, 64], P(('gx', 'gy'))
- down_grad: float32 [4, 4, 4, 64, 64], replicated
Inputs may be any that keep to these rules, and one draw needn't show every extreme that they name: `perf_well`: entry -1 marks an empty slot. Every well appears in exactly 8 slots of one row, the perforations of one vertical well at consecutive depths. Some row has all 256 slots used in every draw. `perf_cell`: local index (x * 8 + y) * 128 + z of the perforated cell in the row's tile of 4 x 8 x 128 coarse cells; 0 in empty slots. `well_slot`: A permutation; row r is held by the device of index r // 16 along gx+gy.
All inputs are finite; a program needn't handle non-finite values.
Results may differ from a plain program's by a relative error of at most 0.0045.
Values may be sent and summed in bfloat16 or wider, within the bound.
No kernel may reach another device: no remote copies, remote signals or barrier semaphores. Data moves between devices by JAX's collectives and lax.ppermute only.
A program may use at most 128 MiB of HBM per device.

v0:
```python
import math

import jax
import jax.numpy as jnp
from jax import lax
from jax.sharding import PartitionSpec as P


def with_halo(array, sides, width):
    for axis, dim in sides:
        devices, length = (lax.axis_size(axis), array.shape[dim])
        up = [(i, (i + 1) % devices) for i in range(devices - 1)]
        down = [(j, i) for i, j in up]
        last = lax.slice_in_dim(array, length - width, length, axis=dim)
        initial = lax.slice_in_dim(array, 0, width, axis=dim)
        before = lax.ppermute(last, axis, up)
        after = lax.ppermute(initial, axis, down)
        array = jnp.concatenate([before, array, after], axis=dim)
    return array


def tile_windows(source, along_dim, pieces, tile_len, margin):
    extent = source.shape
    split_dims = extent[:along_dim] + (pieces, tile_len) + extent[along_dim + 1 :]
    leading_part = lax.slice_in_dim(source, 0, pieces * tile_len, axis=along_dim).reshape(
        split_dims
    )
    trailing = lax.slice_in_dim(source, tile_len, pieces * tile_len + 2 * margin, axis=along_dim)
    padding = [(0, 0)] * source.ndim
    padding[along_dim] = (0, tile_len - 2 * margin)
    trailing = jnp.pad(trailing, padding).reshape(split_dims)
    trailing = lax.slice_in_dim(trailing, 0, 2 * margin, axis=along_dim + 1)
    return jnp.concatenate([leading_part, trailing], axis=along_dim + 1)


def lifting(extended, w_lift, b_lift, out_width, out_height):
    full_depth = extended.shape[3]
    padded = jnp.pad(extended, ((0, 0), (0, 0), (0, 0), (1, 1)))
    channels = w_lift.shape[3]
    outputs = w_lift.shape[4]
    depth_block = min(128, full_depth)
    results = []
    for block_start in range(0, full_depth, depth_block):
        running = jnp.zeros((outputs, out_width, out_height, depth_block), jnp.float32)
        for k in range(3):
            stacked = jnp.concatenate(
                [
                    padded[
                        :,
                        i : i + out_width,
                        j : j + out_height,
                        block_start + k : block_start + k + depth_block,
                    ]
                    for i in range(3)
                    for j in range(3)
                ],
                axis=0,
            )
            kernel_taps = w_lift[:, :, k].reshape(9 * channels, outputs)
            running = running + jnp.einsum(
                "ko,kxyz->oxyz", kernel_taps, stacked, preferred_element_type=jnp.float32
            )
        active = jax.nn.gelu(running + b_lift[:, None, None, None])
        results.append(active.astype(jnp.bfloat16))
    return jnp.concatenate(results, axis=3)


def body(
    fields,
    w_lift,
    b_lift,
    down_weight,
    b_down,
    perf_well,
    perf_cell,
    perf_weight,
    well_slot,
    well_grad,
    field_grad,
):
    grid_gx = lax.axis_size("gx")
    grid_gy = lax.axis_size("gy")
    in_channels, slab_depth, grid_width, grid_height = fields.shape
    tile_width = grid_width // grid_gx
    tile_height = grid_height // grid_gy
    full_depth = slab_depth * grid_gx * grid_gy
    features = w_lift.shape[4]
    margin = 1
    padded = jnp.pad(fields, ((0, 0), (0, 0), (margin, margin), (margin, margin)))
    blocks = tile_windows(
        tile_windows(padded, 2, grid_gx, tile_width, margin), 4, grid_gy, tile_height, margin
    )
    blocks = jnp.transpose(blocks, (2, 4, 0, 1, 3, 5))
    arrived = lax.all_to_all(
        blocks.reshape((grid_gx * grid_gy,) + blocks.shape[2:]),
        ("gx", "gy"),
        split_axis=0,
        concat_axis=0,
        tiled=True,
    )
    arrived = arrived.reshape(blocks.shape)
    columns = jnp.transpose(arrived, (2, 4, 5, 0, 1, 3)).reshape(
        in_channels, tile_width + 2 * margin, tile_height + 2 * margin, full_depth
    )
    hidden = lifting(columns, w_lift, b_lift, tile_width, tile_height)
    rimmed = with_halo(hidden, (("gx", 1), ("gy", 2)), 1)
    half_width = tile_width // 2
    half_height = tile_height // 2
    half_depth = full_depth // 2
    cell_count = half_width * half_height * half_depth
    well_count = well_slot.shape[0]
    listed = perf_well[0]
    cell_ids = perf_cell[0]
    weights = perf_weight[0]
    matches = listed[:, None] == jnp.arange(well_count, dtype=jnp.int32)[None, :]
    out_slots = jnp.sum(jnp.where(matches, well_slot[None, :], 0), axis=1)
    out_slots = jnp.where(listed >= 0, out_slots, -1)
    share_fraction = lax.all_gather(well_grad, ("gx", "gy"), axis=0, tiled=True)
    chosen = out_slots[:, None] == jnp.arange(share_fraction.shape[0], dtype=jnp.int32)[None, :]
    pulled = jnp.dot(
        chosen.astype(jnp.bfloat16), share_fraction, preferred_element_type=jnp.float32
    )
    spread = pulled * weights[:, None]
    flat_grad = field_grad.astype(jnp.float32).reshape(features, cell_count)
    flat_grad = flat_grad.at[:, cell_ids].add(spread.T)
    cotangent = flat_grad.astype(jnp.bfloat16).reshape(
        features, half_width, half_height, half_depth
    )
    stretched = jnp.pad(rimmed, ((0, 0), (0, 0), (0, 0), (1, 1)))
    parity = stretched.reshape(features, half_width + 1, 2, half_height + 1, 2, half_depth + 1, 2)
    parity = jnp.transpose(parity, (2, 4, 6, 0, 1, 3, 5)).reshape(
        8 * features, half_width + 1, half_height + 1, half_depth + 1
    )
    split_weight = down_weight.reshape(2, 2, 2, 2, 2, 2, features, features)
    coarse_sum = jnp.zeros((features, half_width, half_height, half_depth), jnp.float32)
    grad_rows = []
    for a in range(2):
        grad_cols = []
        for b in range(2):
            stacked = jnp.concatenate(
                [
                    parity[:, a : a + half_width, b : b + half_height, depth : depth + half_depth]
                    for depth in range(2)
                ],
                axis=0,
            )
            kernel_taps = jnp.transpose(split_weight[a, :, b], (2, 0, 1, 3, 4, 5)).reshape(
                16 * features, features
            )
            coarse_sum = coarse_sum + jnp.einsum(
                "ko,kxyz->oxyz", kernel_taps, stacked, preferred_element_type=jnp.float32
            )
            grad_part = jnp.einsum(
                "oxyz,kxyz->ko", cotangent, stacked, preferred_element_type=jnp.float32
            )
            grad_cols.append(grad_part.reshape(2, 2, 2, 2, features, features))
        grad_rows.append(jnp.stack(grad_cols))
    local_grad = jnp.transpose(jnp.stack(grad_rows), (0, 3, 1, 4, 2, 5, 6, 7)).reshape(
        4, 4, 4, features, features
    )
    coarse = (coarse_sum + b_down[:, None, None, None]).astype(jnp.bfloat16)
    grad_scale = 1.0 / math.sqrt(cell_count * grid_gx * grid_gy)
    down_grad = lax.psum(local_grad, ("gx", "gy")) * grad_scale
    picked = (
        coarse.reshape(features, cell_count)[:, cell_ids].astype(jnp.float32) * weights[None, :]
    )
    chosen = (
        out_slots[None, :]
        == jnp.arange(well_grad.shape[0] * lax.axis_size(("gx", "gy")), dtype=jnp.int32)[:, None]
    )
    well_feat = lax.psum_scatter(
        jnp.dot(chosen.astype(jnp.float32), picked.T, precision=lax.Precision.HIGHEST),
        ("gx", "gy"),
        scatter_dimension=0,
        tiled=True,
    )
    return (coarse, well_feat, down_grad)


def solution(mesh):
    placed = (
        P(None, ("gx", "gy"), None, None),
        P(),
        P(),
        P(),
        P(),
        P(("gx", "gy"), None),
        P(("gx", "gy"), None),
        P(("gx", "gy"), None),
        P(),
        P(("gx", "gy"), None),
        P(None, "gx", "gy", None),
    )
    return jax.shard_map(
        body,
        mesh=mesh,
        in_specs=placed,
        out_specs=(P(None, "gx", "gy", None), P(("gx", "gy"), None), P()),
        check_vma=False,
    )
```

profile of v0, /device:TPU:1, one launch (start us, length us, event | category | flops | bytes accessed | tf_op | source)
XLA Modules:
  0.0 1408.8 jit_solution(12922795237270653496)
XLA Ops:
  11.7 5.0 reshape.132
  16.7 5.0 reshape.131
  21.7 6.9 maximum_bitcast_fusion
  28.6 5.7 copy.394
  34.3 9.4 reshape.192
  43.8 11.5 all-to-all-start
  56.8 15.2 %all-to-all-done = bf16[128,2,1440]{2,1,0:T(2,128)(2,1)S(1)} async-done(((bf16[128,2,1440]{2,1,0:T(2,128)(2,1)}), bf16[128,2,1440]{2,1,0:T(2,128)(2,1)S(1)}, u32[]{:S(2)}, u32[]{:S(2)}) %all-to-all-start) | async-done | bytes 737312 | tf_op jit(solution)/shard_map/all_to_all | solution.py:94
  72.1 8.9 reshape.193
  81.0 5.3 copy.238
  109.0 322.7 %all_gather.3 = bf16[2048,64]{1,0:T(8,128)(2,1)} all-gather(bf16[16,64]{1,0:T(8,128)(2,1)S(1)} %copy-done.22), channel_id=1, replica_groups=mesh['gx'=16,'gy'=8] {'gx','gy'}, dimensions={0}, use_global_device_ids=true | all-gather | bytes 264192 | tf_op jit(solution)/shard_map/all_gather | solution.py:118
  444.1 4.7 scatter_fusion
  453.0 5.5 collective-permute-start.2
  463.3 4.5 pad_maximum_fusion.4
  467.7 11.8 copy.382
  479.5 11.5 pad.24.clone
  491.1 24.0 %reshape.136 = bf16[64,5,2,9,2,129,2]{0,6,5,4,3,2,1:T(2,128)(2,1)} reshape(bf16[64,10,18,258]{0,3,2,1:T(8,128)(2,1)} %pad.24.clone) | data formatting | bytes 11888640 | tf_op jit(solution)/shard_map/reshape | solution.py:130
  515.1 30.6 %copy.282 = bf16[2,2,2,64,5,9,129]{6,3,2,1,0,5,4:T(8,128)(2,1)} copy(bf16[2,2,2,64,5,9,129]{3,2,6,1,5,0,4:T(2,128)(2,1)} %bitcast.188) | data formatting | bytes 11888640 | tf_op jit(solution)/shard_map/transpose | solution.py:131
  545.7 27.7 %fusion.51 = (bf16[512,4,8,128]{3,0,2,1:T(8,128)(2,1)S(1)}, bf16[512,4,8,128]{3,0,2,1:T(8,128)(2,1)S(1)}, bf16[512,4,8,128]{3,0,2,1:T(8,128)(2,1)S(1)}, bf16[512...) fusion(bf16[512,5,9,129]{3,0,2,1:T(8,128)(2,1)} %bitcast.187), kind=kLoop, calls=%fused_computation.145 | loop fusion | bytes 67108864 | tf_op jit(solution)/shard_map/slice | solution.py:142
  573.5 6.7 pad_maximum_fusion.2
  589.5 4.0 pad_maximum_fusion
  593.5 5.7 fusion.59
  603.7 4.7 convolution_add_fusion.2
  619.4 144.2 %all-reduce.7.cloned.1.call-done = f32[4,4,4,64,64]{4,3,2,1,0:T(8,128)} async-done(((f32[4,4,4,64,64]{4,3,2,1,0:T(8,128)}), f32[4,4,4,64,64]{4,3,2,1,0:T(8,128)}) %all-reduce.7.cloned.1.call-update) | async-done | bytes 1048592 | tf_op jit(solution)/shard_map/psum | solution.py:163
  766.9 634.9 %reduce-scatter.2.cloned.1.call-done = f32[16,64]{1,0:T(8,128)} async-done(((f32[2048,64]{1,0:T(8,128)}), f32[16,64]{1,0:T(8,128)}) %reduce-scatter.2.cloned.1.call-update) | async-done | bytes 4112 | tf_op jit(solution)/shard_map/reduce_scatter | solution.py:171
  (144 shorter events, 77.7 us)
Async XLA Ops:
  34.3 21.0 %copy-start.20 = (s32[1,256]{1,0:T(1,128)S(1)}, s32[1,256]{1,0:T(1,128)}, u32[]{:S(2)}) copy-start(s32[1,256]{1,0:T(1,128)} %param.16) | copy-start | bytes 3076
  34.3 21.0 %copy-start.21 = (s32[2048]{0:T(1024)S(1)}, s32[2048]{0:T(1024)}, u32[]{:S(2)}) copy-start(s32[2048]{0:T(1024)} %param.19) | copy-start | bytes 24580
  34.3 21.4 %copy-start.19 = (bf16[3,3,3,8,64]{4,3,2,1,0:T(8,128)(2,1)S(1)}, bf16[3,3,3,8,64]{4,3,2,1,0:T(8,128)(2,1)}, u32[]{:S(2)}) copy-start(bf16[3,3,3,8,64]{4,3,2,1,0:T(8,128)(2,1)} %param.12) | copy-start | bytes 82948
  34.3 21.5 %copy-start.15 = (bf16[4,4,4,64,64]{4,3,2,1,0:T(8,128)(2,1)S(1)}, bf16[4,4,4,64,64]{4,3,2,1,0:T(8,128)(2,1)}, u32[]{:S(2)}) copy-start(bf16[4,4,4,64,64]{4,3,2,1,0:T(8,128)(2,1)} %param.14) | copy-start | bytes 1572868
  43.8 28.3 %all-to-all-start = ((bf16[128,2,1440]{2,1,0:T(2,128)(2,1)}), bf16[128,2,1440]{2,1,0:T(2,128)(2,1)S(1)}, u32[]{:S(2)}, u32[]{:S(2)}) async-start(bf16[128,2,1440]{2,1,0:T(2,128)(2,1)} %reshape.192), calls=%async_computation | async-start | bytes 1572864 | tf_op jit(solution)/shard_map/all_to_all | solution.py:94
  55.3 708.4 %all-reduce.7.cloned.1.call-start = ((), (), s32[]{:S(2)}) async-start(), calls=%async_computation.3 | async-start | bytes 4194304 | tf_op jit(solution)/shard_map/psum | solution.py:163
  101.8 7.2 copy-start.22
  103.4 348.2 %collective-permute-start.1 = (bf16[64,1,16,256]{3,0,2,1:T(8,128)(2,1)}, bf16[64,1,16,256]{3,0,2,1:T(8,128)(2,1)S(1)}, u32[]{:S(2)}, u32[]{:S(2)}) collective-permute-start(bf16[64,1,16,256]{3,0,2,1:T(8,128)(2,1)} %get-tuple-element.29), channel_id=1, source_target_pairs={{8,0},{16,8},{24,16},{32,24},{40,32},{48,40},{56,48},{64,56},{72,6... | collective-permute-start | bytes 1572872 | tf_op jit(solution)/shard_map/ppermute | solution.py:17
  105.3 346.2 %collective-permute-start = (bf16[64,1,16,256]{3,0,2,1:T(8,128)(2,1)}, bf16[64,1,16,256]{3,0,2,1:T(8,128)(2,1)S(1)}, u32[]{:S(2)}, u32[]{:S(2)}) collective-permute-start(bf16[64,1,16,256]{3,0,2,1:T(8,128)(2,1)} %get-tuple-element.28), channel_id=1, source_target_pairs={{0,8},{8,16},{16,24},{24,32},{32,40},{40,48},{48,56},{56,64},{64,7... | collective-permute-start | bytes 1572872 | tf_op jit(solution)/shard_map/ppermute | solution.py:16
  437.2 6.9 copy-start.23
  451.7 9.3 collective-permute-start.3
  453.0 10.3 collective-permute-start.2
  573.4 6.7 copy-start.2
  573.4 6.7 copy-start.4
  573.4 6.7 copy-start.6
  573.4 6.7 copy-start.13
  586.0 3.5 copy-start.10
  589.5 4.0 copy-start.14
  603.6 798.2 %reduce-scatter.2.cloned.1.call-start = ((), (), s32[]{:S(2)}) async-start(), calls=%async_computation.2 | async-start | bytes 1056768 | tf_op jit(solution)/shard_map/reduce_scatter | solution.py:171
  603.7 4.7 copy-start.7
  603.7 5.9 copy-start.8
  609.6 3.5 copy-start.5
  609.6 3.5 copy-start.16
  609.6 3.5 copy-start.26
  (10 other events, 23.8 us)
Sparse Core Ops, SparseCore 0:
  603.7 159.8 all-reduce.6
  766.6 635.2 reduce-scatter.1
where the time goes:
time: 1430 us; the launch traced here: 1410 us
  waiting for transfers between devices  799 us (56%)
  blocking collectives  323 us (23%)
  local copies, waits for them, and re-layouts  178 us (12%)
  other arithmetic  35.1 us (2%)
  matrix products  34.7 us (2%)
  starting transfers between devices  23.9 us (2%)
  between operations  15 us (1%)
    reduce_scatter x1, waiting for transfers between devices, body(): lax.psum_scatter(jnp.dot(chosen.astype(jnp.float32), picked.T, precision=...  635 us
    all_gather x1, blocking collectives, body(): share_fraction = lax.all_gather(well_grad, ('gx', 'gy'), axis=0, tiled=True)  323 us
    psum x1, waiting for transfers between devices, body(): down_grad = lax.psum(local_grad, ('gx', 'gy')) * grad_scale  144 us
    unnamed x83, local copies, waits for them, and re-layouts  47.9 us
    transpose x1, local copies, waits for them, and re-layouts, body(): jnp.transpose(parity, (2, 4, 6, 0, 1, 3, 5))  30.6 us
  transfers between devices with their start and end apart: 7, of which 5 were waited for; matrix products, arithmetic and copies ran while one was open for 3% of the time, Pallas kernels for 0%

commit v1 on v0

v1 whole, which is shorter than its diff:
```python
import math

import jax
import jax.numpy as jnp
from jax import lax
from jax.experimental import pallas as pl
from jax.experimental.pallas import tpu as pltpu
from jax.sharding import PartitionSpec as P

BF = jnp.bfloat16
F32 = jnp.float32
I32 = jnp.int32
AXES = ("gx", "gy")
INTERPRET = False
ROOT_2_PI = math.sqrt(2.0 / math.pi)


def dot_nn(a, b):
    return lax.dot_general(a, b, (((1,), (0,)), ((), ())), preferred_element_type=F32)


def dot_nt(a, b):
    return lax.dot_general(a, b, (((1,), (1,)), ((), ())), preferred_element_type=F32)


def iota(shape, dim):
    return lax.broadcasted_iota(I32, shape, dim)


def ones_where(mask):
    return jnp.where(mask, 1.0, 0.0).astype(BF)


def split(x):
    high = x.astype(BF)
    return high, (x - high.astype(F32)).astype(BF)


def pack_kernel(fields_ref, wells_ref, out_ref):
    lane = iota((1, 1024), 1)
    within = lane & 127
    which = (within * 205) >> 12
    y = (lane >> 7) * 16 - 2 + within - 20 * which
    target = jnp.where((which < 6) & (y >= 0) & (y < 128), which * 128 + y, -1)
    spread = ones_where(iota((768, 1024), 0) == target)
    row, col = iota((256, 144), 0), iota((256, 144), 1)
    xx = row & 15
    windows = ones_where(
        ((xx < 12) & (col < 128) & (col == (row >> 4) * 8 - 2 + xx))
        | ((xx >= 12) & (col - 128 == xx))
    )
    empty = jnp.zeros((128, 128), BF)
    for group in range(3):
        planes = [
            fields_ref[6 * group + j] if 6 * group + j < 16 else empty for j in range(6)
        ]
        lined = dot_nn(jnp.concatenate(planes, axis=1), spread).astype(BF)
        if group < 2:
            piece = wells_ref[:, 128 * group : 128 * group + 128]
        else:
            piece = jnp.zeros((16, 128), BF)
        lined = jnp.concatenate([lined, jnp.concatenate([piece] * 8, axis=1)], axis=0)
        blocks = dot_nn(windows, lined).astype(BF).reshape(16, 16, 1024)
        for b in range(8):
            out_ref[:, b, :, 128 * group : 128 * group + 128] = blocks[
                :, :, 128 * b : 128 * b + 128
            ]


def prep_kernel(
    well_ref,
    cell_ref,
    table_ref,
    lift_ref,
    down_ref,
    field_ref,
    cells_ref,
    rows_ref,
    quarter_ref,
    owner_ref,
    lanes_ref,
    big_ref,
    taps_ref,
    grad_ref,
):
    well = well_ref[...]
    used = well >= 0
    cells_ref[...] = ones_where(iota((4096, 256), 0) == jnp.where(used, cell_ref[...], -1))
    matches = ones_where(iota((2048, 256), 0) == well)
    table = table_ref[...]
    row = iota((8, 2048), 0)
    digits = jnp.where(row == 0, table >> 4, jnp.where(row == 1, table & 15, 0))
    found = dot_nn(digits.astype(F32).astype(BF), matches)
    slot = jnp.where(used, (found[0:1] * 16.0 + found[1:2]).astype(I32), -1)
    for half in range(2):
        place = jnp.where(
            used & (((slot >> 3) & 1) == half), (slot >> 4) * 8 + (slot & 7), -1
        )
        owner_ref[:, 256 * half : 256 * half + 256] = ones_where(iota((1024, 256), 0) == place)
    column = jnp.transpose(jnp.broadcast_to(slot, (128, 256)).astype(F32))[:, 0:1].astype(I32)
    place = jnp.where(column >= 0, ((column >> 2) & 3) * 128 + (column >> 4), -1)
    rows_ref[...] = ones_where(iota((256, 512), 1) == place)
    quarter_ref[...] = jnp.where((iota((256, 256), 1) >> 6) == (column & 3), 1.0, 0.0)

    lane = iota((1, 1152), 1)
    plane = lane & 15
    group = (plane * 43) >> 8
    target = (
        ((lane >> 4) & 1) * 384
        + group * 128
        + (plane - 6 * group) * 20
        + 2 * (lane >> 7)
        + ((lane >> 5) & 3)
    )
    lanes_ref[...] = ones_where(iota((768, 1152), 0) == target)

    row = iota((256, 1), 0)
    x = 2 * (row >> 7) + ((row >> 4) & 1)
    y = (row >> 5) & 3
    channel = (row >> 1) & 7
    col = iota((256, 256), 1)
    for ds in range(2):
        z = 2 * ds + (row & 1)
        for px in range(2):
            for py in range(2):
                parts = []
                for pz in range(2):
                    i, j, k = x - px, y - py, z - pz
                    good = (i >= 0) & (i < 3) & (j >= 0) & (j < 3) & (k >= 0) & (k < 3)
                    tap = jnp.where(good, ((i * 3 + j) * 3 + k) * 8 + channel, -1)
                    parts.append(ones_where(col == tap))
                block = dot_nn(jnp.concatenate(parts, axis=1), lift_ref[...])
                at = ds * 512 + (px * 2 + py) * 128
                big_ref[:, at : at + 128] = block.astype(BF)

    eye = ones_where(iota((64, 64), 0) == iota((64, 64), 1))
    turned = dot_nt(eye, down_ref[...]).astype(BF)
    for a in range(2):
        for b in range(2):
            for d in range(2):
                for p in range(4):
                    at = ((2 * a + p // 2) * 4 + 2 * b + p % 2) * 256 + d * 128
                    taps_ref[2 * a + b, 64 * d : 64 * d + 64, 128 * p : 128 * p + 128] = turned[
                        :, at : at + 128
                    ]

    row, col = iota((256, 256), 0), iota((256, 256), 1)
    turn = ones_where(col == (row & 7) * 32 + (row >> 3))
    for g in range(8):
        part = dot_nn(turn, field_ref[8 * g : 8 * g + 8].reshape(256, 128))
        for uv in range(32):
            grad_ref[8 * g : 8 * g + 8, 128 * uv : 128 * uv + 128] = part[
                8 * uv : 8 * uv + 8
            ]


def lift_kernel(
    tile_ref,
    arrived_ref,
    weight_ref,
    bias_ref,
    cells_ref,
    rows_ref,
    quarter_ref,
    lanes_ref,
    big_ref,
    grad_ref,
    send_ref,
    pairs_ref,
    last_ref,
    sorted_ref,
    wells_ref,
    window_ref,
    raw_ref,
    tail_ref,
    cot_ref,
    sum_ref,
):
    a, b = tile_ref[0], tile_ref[1]

    row, col = iota((256, 256), 0), iota((256, 256), 1)
    place = row >> 4
    x = jnp.where(place < 6, 2 * place, jnp.where(place < 12, 2 * place - 11, place))
    turn = ones_where(col == (row & 15) * 16 + x)

    def sort(g, carry):
        block = arrived_ref[pl.ds(16 * g, 16)].reshape(256, 384)
        part = dot_nn(turn, block).astype(BF)
        for xp in range(2):
            for x2 in range(6):
                at = 16 * (6 * xp + x2)
                sorted_ref[
                    pl.ds(pl.multiple_of(128 * x2 + 16 * g, 16), 16), 384 * xp : 384 * xp + 384
                ] = part[at : at + 16]
        for t in range(4):
            wells_ref[pl.ds(pl.multiple_of(128 * t + 16 * g, 16), 16), :] = part[
                192 + 16 * t : 208 + 16 * t, 0:256
            ]
        return carry

    lax.fori_loop(0, 8, sort, 0)

    def lanes(x2, carry):
        at = pl.multiple_of(128 * x2, 128)
        part = dot_nn(sorted_ref[pl.ds(at, 128), :], lanes_ref[...]).astype(BF)
        for v in range(9):
            window_ref[v, pl.ds(at, 128), :] = part[:, 128 * v : 128 * v + 128]
        return carry

    lax.fori_loop(0, 6, lanes, 0)

    lane = iota((64, 256), 1)
    fold = ones_where((lane & 63) == iota((64, 256), 0))
    pulled = (dot_nn(rows_ref[...], wells_ref[...]) * quarter_ref[...]).astype(BF)
    spread = dot_nt(fold, pulled) * weight_ref[...]
    added = dot_nt(jnp.concatenate(split(spread), axis=0), cells_ref[...])
    grown = (grad_ref[...] + added[0:64] + added[64:128]).astype(BF)
    cot_ref[0:64, :] = grown
    lane = iota((64, 128), 1)
    ends = jnp.zeros((64, 128), F32)
    for uv in range(32):
        piece = grown[:, 128 * uv : 128 * uv + 128].astype(F32)
        moved = pltpu.roll(piece, 1, 1)
        cot_ref[64:128, 128 * uv : 128 * uv + 128] = jnp.where(lane == 0, 0.0, moved).astype(BF)
        at = (uv // 8) * 9 + uv % 8
        ends = jnp.where(lane == at, pltpu.roll(piece, at + 1, 1), ends)

    lane = iota((1, 512), 1)
    px, py, pz = lane >> 8, (lane >> 7) & 1, (lane >> 6) & 1
    bias = bias_ref[...]

    def active(v):
        return 0.5 * v * (1.0 + jnp.tanh(ROOT_2_PI * (v + 0.044715 * (v * v * v))))

    def inside(u, v):
        left = jnp.where((a == 0) & (u == 0), 0.0, 1.0)
        right = jnp.where((a == 15) & (u == 4), 0.0, 1.0)
        low = jnp.where((b == 0) & (v == 0), 0.0, 1.0)
        high = jnp.where((b == 7) & (v == 8), 0.0, 1.0)
        return jnp.where(px == 0, left, right) * jnp.where(py == 0, low, high)

    tail_ref[...] = jnp.zeros((128, 512), F32)
    first = iota((128, 512), 0) == 0
    start = jnp.where(first & (pz == 0), 0.0, 1.0)

    def strip(v, carry):
        window = window_ref[v]
        both = jnp.concatenate([window[0:640], window[128:768]], axis=1)
        raw_ref[...] = dot_nn(both, big_ref[...])

        def cell(u, inner):
            at = pl.multiple_of(128 * u, 128)
            before = raw_ref[pl.ds(at, 128), 0:512]
            after = raw_ref[pl.ds(at, 128), 512:1024]
            keep = inside(u, v)
            ending = active(before[127:128] + bias) * keep * jnp.where(pz == 0, 1.0, 0.0)
            tail_ref[pl.ds(u * 9 + v, 1), :] = ending
            moved = jnp.where(first, 0.0, pltpu.roll(before, 1, 0))
            value = active(moved + after + bias) * (keep * start)
            pairs_ref[u, v] = value.astype(BF)
            return inner

        return lax.fori_loop(0, 5, cell, carry)

    lax.fori_loop(0, 9, strip, 0)
    last = tail_ref[...].astype(BF)
    last_ref[...] = last

    sum_ref[...] = jnp.zeros((512, 512), F32)
    for i in range(2):
        for j in range(2):
            shift = 9 * i + j
            edge = (pltpu.roll(ends, shift, 1) if shift else ends).astype(BF)
            at = 128 * (2 * i + j) + 64
            sum_ref[at : at + 64, :] = dot_nn(edge, last)

    def gather(u, carry):
        cot = cot_ref[:, pl.ds(pl.multiple_of(1024 * u, 1024), 1024)]
        for i in range(2):
            for j in range(2):
                group = pairs_ref[u + i, j : j + 8].reshape(1024, 512)
                at = 128 * (2 * i + j)
                sum_ref[at : at + 128, :] += dot_nn(cot, group)
        return carry

    lax.fori_loop(0, 4, gather, 0)
    for r in range(32):
        for j in range(4):
            send_ref[4 * r + j] = sum_ref[16 * r : 16 * r + 16, 128 * j : 128 * j + 128].astype(BF)


def coarse_kernel(
    pairs_ref,
    last_ref,
    taps_ref,
    bias_ref,
    weight_ref,
    cells_ref,
    owner_ref,
    coarse_ref,
    feat_ref,
    wide_ref,
):
    lane = iota((64, 128), 1)
    edge = jnp.zeros((64, 128), F32)
    for i in range(2):
        for j in range(2):
            part = dot_nt(taps_ref[2 * i + j, 64:128, :], last_ref[...])
            shift = (128 - 9 * i - j) % 128
            edge = edge + (pltpu.roll(part, shift, 1) if shift else part)
    bias = bias_ref[...]

    def layer(u, carry):
        total = None
        for i in range(2):
            for j in range(2):
                group = pairs_ref[u + i, j : j + 8].reshape(1024, 512)
                part = dot_nt(taps_ref[2 * i + j], group)
                total = part if total is None else total + part
        for v in range(8):
            near = total[0:64, 128 * v : 128 * v + 128]
            deep = pltpu.roll(total[64:128, 128 * v : 128 * v + 128], 127, 1)
            end = pltpu.roll(edge, 127 - (9 * u + v), 1)
            value = near + jnp.where(lane == 127, end, deep) + bias
            at = pl.multiple_of(1024 * u + 128 * v, 128)
            wide_ref[:, pl.ds(at, 128)] = value
        return carry

    lax.fori_loop(0, 4, layer, 0)

    picked = dot_nn(wide_ref[...].astype(BF), cells_ref[...]) * weight_ref[...]
    feat = jnp.zeros((1024, 128), F32)
    none = jnp.zeros((64, 256), BF)
    for part in split(picked):
        twice = jnp.concatenate(
            [jnp.concatenate([part, none], axis=1), jnp.concatenate([none, part], axis=1)], axis=0
        )
        feat = feat + dot_nt(owner_ref[...], twice)
    feat_ref[...] = feat.astype(BF).reshape(128, 8, 128)

    row, col = iota((256, 256), 0), iota((256, 256), 1)
    turn = ones_where(col == (row & 31) * 8 + (row >> 5))
    for g in range(8):
        tall = jnp.concatenate(
            [wide_ref[8 * g : 8 * g + 8, 128 * uv : 128 * uv + 128] for uv in range(32)], axis=0
        )
        part = dot_nn(turn, tall.astype(BF)).astype(BF)
        coarse_ref[8 * g : 8 * g + 8] = part.reshape(8, 32, 128)


def sum_kernel(scale, parts_ref, feat_ref, out_ref):
    total = jnp.sum(parts_ref[...].astype(F32), axis=0) * scale
    out_ref[:, 0:16, :] = jnp.broadcast_to(total.astype(BF)[None], (128, 16, 128))
    out_ref[:, 16:24, :] = feat_ref[...]


def finish_kernel(arrived_ref, grad_ref, feat_ref):
    eye = ones_where(iota((128, 128), 0) == iota((128, 128), 1))
    for a in range(2):
        for b in range(2):
            for d in range(2):
                base = 4 * (4 * a + 2 * b + d)
                for p in range(4):
                    block = jnp.concatenate(
                        [arrived_ref[4 * (base + t) + p, 0:16, :] for t in range(4)], axis=0
                    )
                    tap = ((2 * a + p // 2) * 4 + 2 * b + p % 2) * 4 + 2 * d
                    grad_ref[64 * tap : 64 * tap + 128, :] = dot_nt(eye, block)
    feat = jnp.sum(arrived_ref[:, 16:24, :].astype(F32), axis=0)
    feat_ref[0:8, :] = feat[:, 0:64]
    feat_ref[8:16, :] = pltpu.roll(feat, 64, 1)[:, 0:64]


def call(kernel, outs, scratch=(), scalars=0, cost=0):
    extra = {}
    if scalars:
        extra["in_specs"] = [pl.BlockSpec(memory_space=pltpu.SMEM)] + [
            pl.BlockSpec(memory_space=pltpu.VMEM)
        ] * scalars
    return pl.pallas_call(
        kernel,
        out_shape=[jax.ShapeDtypeStruct(shape, dtype) for shape, dtype in outs],
        scratch_shapes=[pltpu.VMEM(shape, dtype) for shape, dtype in scratch],
        compiler_params=pltpu.CompilerParams(vmem_limit_bytes=56 << 20),
        cost_estimate=pl.CostEstimate(flops=cost, bytes_accessed=1 << 20, transcendentals=0),
        interpret=INTERPRET,
        **extra,
    )


def pack(fields, well_grad):
    wells = jnp.pad(well_grad.reshape(4, 256), ((12, 0), (0, 0)))
    return call(pack_kernel, [((16, 8, 16, 384), BF)], cost=1 << 31)(
        fields.reshape(16, 128, 128), wells
    )[0].reshape(128, 16, 384)


def prepare(perf_well, perf_cell, well_slot, w_lift, down_weight, field_grad):
    flat = jnp.pad(w_lift.reshape(216, 64), ((0, 40), (0, 0)))
    none = jnp.zeros_like(flat)
    lift = jnp.concatenate(
        [jnp.concatenate([flat, none], axis=1), jnp.concatenate([none, flat], axis=1)], axis=0
    )
    outs = [
        ((4096, 256), BF),
        ((256, 512), BF),
        ((256, 256), F32),
        ((1024, 512), BF),
        ((768, 1152), BF),
        ((256, 1024), BF),
        ((4, 128, 512), BF),
        ((64, 4096), F32),
    ]
    return call(prep_kernel, outs, cost=1 << 32)(
        perf_well,
        perf_cell,
        well_slot.reshape(1, 2048),
        lift,
        down_weight.reshape(4096, 64),
        field_grad.reshape(64, 32, 128),
    )


def lift(tile, arrived, perf_weight, b_lift, cells, rows, quarter, lanes, big, grad):
    outs = [((128, 16, 128), BF), ((5, 9, 128, 512), BF), ((128, 512), BF)]
    scratch = [
        ((768, 768), BF),
        ((512, 256), BF),
        ((9, 768, 128), BF),
        ((640, 1024), F32),
        ((128, 512), F32),
        ((128, 4096), BF),
        ((512, 512), F32),
    ]
    return call(lift_kernel, outs, scratch, scalars=9, cost=1 << 33)(
        tile,
        arrived,
        perf_weight,
        jnp.tile(b_lift, 8)[None, :],
        cells,
        rows,
        quarter,
        lanes,
        big,
        grad,
    )


def coarsen(pairs, last, taps, b_down, perf_weight, cells, owner):
    outs = [((64, 32, 128), BF), ((128, 8, 128), BF)]
    return call(coarse_kernel, outs, [((64, 4096), F32)], cost=1 << 33)(
        pairs, last, taps, b_down[:, None], perf_weight, cells, owner
    )


def exchange(blocks):
    return lax.all_to_all(blocks, AXES, split_axis=0, concat_axis=0, tiled=True)


def body(
    fields,
    w_lift,
    b_lift,
    down_weight,
    b_down,
    perf_well,
    perf_cell,
    perf_weight,
    well_slot,
    well_grad,
    field_grad,
):
    scale = 1.0 / math.sqrt(64 * 64 * 128)
    tile = jnp.stack([lax.axis_index("gx"), lax.axis_index("gy")]).astype(I32)
    arrived = exchange(pack(fields, well_grad))
    cells, rows, quarter, owner, lanes, big, taps, grad = prepare(
        perf_well, perf_cell, well_slot, w_lift, down_weight, field_grad
    )
    parts, pairs, last = lift(
        tile, arrived, perf_weight, b_lift, cells, rows, quarter, lanes, big, grad
    )
    parts = exchange(parts)
    coarse, feat = coarsen(pairs, last, taps, b_down, perf_weight, cells, owner)
    shared = call(
        lambda *refs: sum_kernel(scale, *refs), [((128, 24, 128), BF)], cost=1 << 20
    )(parts, feat)[0]
    shared = exchange(shared)
    down_grad, well_feat = call(
        finish_kernel, [((4096, 64), F32), ((16, 64), F32)], cost=1 << 28
    )(shared)
    return (
        coarse.reshape(64, 4, 8, 128),
        well_feat,
        down_grad.reshape(4, 4, 4, 64, 64),
    )


def solution(mesh):
    placed = (
        P(None, AXES, None, None),
        P(),
        P(),
        P(),
        P(),
        P(AXES, None),
        P(AXES, None),
        P(AXES, None),
        P(),
        P(AXES, None),
        P(None, "gx", "gy", None),
    )
    return jax.shard_map(
        body,
        mesh=mesh,
        in_specs=placed,
        out_specs=(P(None, "gx", "gy", None), P(AXES, None), P()),
        check_vma=False,
    )
```

time: 1430 us -> 119 us (0.08); the launches traced: 1410 us -> 119 us
  waiting for transfers between devices: 799 us -> 16 us
  blocking collectives: 323 us -> 25.8 us
  local copies, waits for them, and re-layouts: 178 us -> 4.81 us
  Pallas kernels: 0 us -> 54.5 us
  matrix products: 34.7 us -> 0 us
  other arithmetic: 35.1 us -> 1.33 us
  between operations: 15 us -> 0.7 us
    reduce_scatter x1 -> x0, waiting for transfers between devices: 635 us -> none  [body(): lax.psum_scatter(jnp.dot(chosen.astype(jnp.float32), picked.T, precision=...]
    all_gather x1 -> x0, blocking collectives: 323 us -> none  [body(): share_fraction = lax.all_gather(well_grad, ('gx', 'gy'), axis=0, tiled=True)]
    psum x1 -> x0, waiting for transfers between devices: 144 us -> none  [body(): down_grad = lax.psum(local_grad, ('gx', 'gy')) * grad_scale]
    pallas_call x0 -> x6, Pallas kernels: none -> 54.5 us  [the longest x1 25.4 us: lift(): call(lift_kernel, outs, scratch, scalars=9, cost=1 << 33)]
    reshape x13 -> x1, local copies, waits for them, and re-layouts: 53.2 us -> 0.77 us  [pack(): wells = jnp.pad(well_grad.reshape(4, 256), ((12, 0), (0, 0)))]
    unnamed x83 -> x10, local copies, waits for them, and re-layouts: 47.9 us -> 2.04 us
    dot_general x16 -> x0, matrix products: 34.7 us -> none  [the longest x4 12.7 us: body(): jnp.einsum('oxyz,kxyz->ko', cotangent, stacked, preferred_element_type=jn...]
    transpose x2 -> x0, local copies, waits for them, and re-layouts: 32 us -> none  [the longest x1 30.6 us: body(): jnp.transpose(parity, (2, 4, 6, 0, 1, 3, 5))]
  transfers between devices with their start and end apart: 7 -> 2, of which waited for: 5 -> 2; matrix products, arithmetic and copies ran while one was open for 3% -> 2% of each run, Pallas kernels for 0% -> 17%
where the time goes in v1:
time: 119 us
  Pallas kernels  54.5 us (46%)
  blocking collectives  25.8 us (22%)
  waiting for transfers between devices  16 us (13%)
  starting transfers between devices  15.4 us (13%)
  local copies, waits for them, and re-layouts  4.81 us (4%)
  other arithmetic  1.33 us (1%)
    all_to_all x1, blocking collectives, exchange(): return lax.all_to_all(blocks, AXES, split_axis=0, concat_axis=0, tiled=True)  25.8 us
    pallas_call x1, Pallas kernels, lift(): call(lift_kernel, outs, scratch, scalars=9, cost=1 << 33)  25.4 us
    all_to_all x2, waiting for transfers between devices, exchange(): return lax.all_to_all(blocks, AXES, split_axis=0, concat_axis=0, tiled=True)  16 us
    all_to_all x2, starting transfers between devices, exchange(): return lax.all_to_all(blocks, AXES, split_axis=0, concat_axis=0, tiled=True)  15.4 us
    pallas_call x1, Pallas kernels, coarsen(): call(coarse_kernel, outs, [((64, 4096), F32)], cost=1 << 33)  13.2 us
    pallas_call x1, Pallas kernels, prepare(): call(prep_kernel, outs, cost=1 << 32)  7.21 us
    pallas_call x1, Pallas kernels, pack(): call(pack_kernel, [((16, 8, 16, 384), BF)], cost=1 << 31)  3.76 us
    pallas_call x1, Pallas kernels, body(): call(finish_kernel, [((4096, 64), F32), ((16, 64), F32)], cost=1 << 28)  2.88 us
  transfers between devices with their start and end apart: 2, of which 2 were waited for; matrix products, arithmetic and copies ran while one was open for 2% of the time, Pallas kernels for 17%

profile of v1, /device:TPU:1, one launch (start us, length us, event | category | flops | bytes accessed | tf_op | source)
XLA Modules:
  0.0 118.6 jit_solution(9969109056482328349)
XLA Ops:
  0.6 0.8 reshape.35
  1.4 0.6 pad.10.wells_ref
  2.0 3.8 %shard_map.130 = bf16[16,8,16,384]{3,2,1,0:T(8,128)(2,1)} custom-call(bf16[16,128,128]{2,1,0:T(8,128)(2,1)} %bitcast.15, bf16[16,256]{1,0:T(8,128)(2,1)} %pad.10.wells_ref), custom_call_target="tpu_custom_call" | custom-call | flops 2147483648 | bytes 1048576 | tf_op jit(solution)/shard_map/pallas_call | solution.py:393
  5.8 0.0 copy-start.2
  5.8 0.0 copy-start.3
  5.8 11.5 %all-to-all-start = ((bf16[128,16,384]{2,1,0:T(8,128)(2,1)}), bf16[128,16,384]{2,1,0:T(8,128)(2,1)S(1)}, u32[]{:S(2)}, u32[]{:S(2)}) async-start(bf16[128,16,384]{2,1,0:T(8,128)(2,1)} %bitcast.11), calls=%async_computation | async-start | bytes 3145728 | tf_op jit(solution)/shard_map/all_to_all | solution.py:457
  17.3 0.0 copy-done.2
  17.3 0.0 copy-done.4
  17.3 0.7 broadcast_in_dim_tile.3.bias_ref
  18.0 0.0 copy-done.3
  18.0 0.7 copy.14.bias_ref
  18.7 0.6 pad_add_fusion.tile_ref
  19.3 0.7 fusion.2.lift_ref
  20.0 7.2 %shard_map.131 = (bf16[4096,256]{1,0:T(8,128)(2,1)}, bf16[256,512]{1,0:T(8,128)(2,1)}, f32[256,256]{1,0:T(8,128)}, bf16[1024,512]{1,0:T(8,128)(2,1)}, bf16[768,1...) custom-call(s32[1,256]{1,0:T(1,128)} %well_ref.1, ...), custom_call_target="tpu_custom_call" | custom-call | flops 4294967296 | bytes 1048576 | tf_op jit(solution)/shard_map/pallas_call | solution.py:414
  27.3 15.1 %all-to-all-done.arrived_ref = bf16[128,16,384]{2,1,0:T(8,128)(2,1)S(1)} async-done(((bf16[128,16,384]{2,1,0:T(8,128)(2,1)}), bf16[128,16,384]{2,1,0:T(8,128)(2,1)S(1)}, u32[]{:S(2)}, u32[]{:S(2)}) %all-to-all-start) | async-done | bytes 1572896 | tf_op jit(solution)/shard_map/all_to_all | solution.py:457
  42.4 1.2 %copy-done.1 = bf16[128,16,384]{2,1,0:T(8,128)(2,1)} copy-done((bf16[128,16,384]{2,1,0:T(8,128)(2,1)}, bf16[128,16,384]{2,1,0:T(8,128)(2,1)S(1)}, u32[]{:S(2)}) %copy-start.1) | copy-done | bytes 1572888
  43.6 25.4 %shard_map.132 = (bf16[128,16,128]{2,1,0:T(8,128)(2,1)}, bf16[5,9,128,512]{3,2,1,0:T(8,128)(2,1)}, bf16[128,512]{1,0:T(8,128)(2,1)}) custom-call(s32[2]{0:T(128)} %pad_add_fusion.tile_ref, bf16[128,16,384]{2,1,0:T(8,128)(2,1)} %copy-done.1, f32[1,256]{1,0:T(1,128)} %weight_ref.3, f32[1,512]{1,0:T(1,128)} %broadcast_in_dim_tile.3.bias_ref, ...), custom_call_target="tpu_custom_call" | custom-call | flops 8589934592 | bytes 1048576 | tf_op jit(solution)/shard_map/pallas_call | solution.py:435
  69.0 4.0 %all-to-all-start.1 = ((bf16[128,16,128]{2,1,0:T(8,128)(2,1)}), bf16[128,16,128]{2,1,0:T(8,128)(2,1)S(1)}, u32[]{:S(2)}, u32[]{:S(2)}) async-start(bf16[128,16,128]{2,1,0:T(8,128)(2,1)} %get-tuple-element.29), calls=%async_computation.1 | async-start | bytes 1048576 | tf_op jit(solution)/shard_map/all_to_all | solution.py:457
  72.9 13.2 %shard_map.133 = (bf16[64,32,128]{2,1,0:T(8,128)(2,1)}, bf16[128,8,128]{2,1,0:T(8,128)(2,1)}) custom-call(bf16[5,9,128,512]{3,2,1,0:T(8,128)(2,1)} %get-tuple-element.24.pairs_ref, bf16[128,512]{1,0:T(8,128)(2,1)} %get-tuple-element.25.last_ref, bf16[4,128,512]{2,1,0:T(8,128)(2,1)} %get-tuple-element.26.taps_ref, f32[64,1]{1,0:T(8,128)} %copy.14.bias_ref, ...), custom_call_target="tpu_custom_call" | custom-call | flops 8589934592 | bytes 1048576 | tf_op jit(solution)/shard_map/pallas_call | solution.py:451
  86.1 0.9 all-to-all-done.1.refs_0_
  87.0 0.8 copy-done
  87.8 2.2 %shard_map.134 = bf16[128,24,128]{2,1,0:T(8,128)(2,1)} custom-call(bf16[128,16,128]{2,1,0:T(8,128)(2,1)} %copy-done, bf16[128,8,128]{2,1,0:T(8,128)(2,1)} %get-tuple-element.30.refs_1_), custom_call_target="tpu_custom_call" | custom-call | flops 1048576 | bytes 1048576 | tf_op jit(solution)/shard_map/pallas_call | solution.py:484
  90.0 25.8 %all_to_all.15.arrived_ref = bf16[128,24,128]{2,1,0:T(8,128)(2,1)} all-to-all(bf16[128,24,128]{2,1,0:T(8,128)(2,1)} %shard_map.134), channel_id=1, replica_groups=mesh['gx'=16,'gy'=8] {'gx','gy'}, dimensions={0} | all-to-all | bytes 1572864 | tf_op jit(solution)/shard_map/all_to_all | solution.py:457
  115.8 2.9 %shard_map.135 = (f32[4096,64]{1,0:T(8,128)}, f32[16,64]{1,0:T(8,128)}) custom-call(bf16[128,24,128]{2,1,0:T(8,128)(2,1)} %all_to_all.15.arrived_ref), custom_call_target="tpu_custom_call" | custom-call | flops 268435456 | bytes 1048576 | tf_op jit(solution)/shard_map/pallas_call | solution.py:488
  (5 shorter events, 0.0 us)
Async XLA Ops:
  5.8 11.5 %copy-start.2 = (bf16[3,3,3,8,64]{4,3,2,1,0:T(8,128)(2,1)S(1)}, bf16[3,3,3,8,64]{4,3,2,1,0:T(8,128)(2,1)}, u32[]{:S(2)}) copy-start(bf16[3,3,3,8,64]{4,3,2,1,0:T(8,128)(2,1)} %param.12) | copy-start | bytes 82948
  5.8 11.5 %copy-start.4 = (f32[64]{0:T(128)S(1)}, f32[64]{0:T(128)}, u32[]{:S(2)}) copy-start(f32[64]{0:T(128)} %param.13) | copy-start | bytes 772
  5.8 12.2 %copy-start.3 = (f32[64]{0:T(128)S(1)}, f32[64]{0:T(128)}, u32[]{:S(2)}) copy-start(f32[64]{0:T(128)} %param.15) | copy-start | bytes 772
  5.8 36.6 %all-to-all-start = ((bf16[128,16,384]{2,1,0:T(8,128)(2,1)}), bf16[128,16,384]{2,1,0:T(8,128)(2,1)S(1)}, u32[]{:S(2)}, u32[]{:S(2)}) async-start(bf16[128,16,384]{2,1,0:T(8,128)(2,1)} %bitcast.11), calls=%async_computation | async-start | bytes 3145728 | tf_op jit(solution)/shard_map/all_to_all | solution.py:457
  42.4 1.2 %copy-start.1 = (bf16[128,16,384]{2,1,0:T(8,128)(2,1)}, bf16[128,16,384]{2,1,0:T(8,128)(2,1)S(1)}, u32[]{:S(2)}) copy-start(bf16[128,16,384]{2,1,0:T(8,128)(2,1)S(1)} %all-to-all-done.arrived_ref) | copy-start | bytes 4718596
  69.0 18.0 %all-to-all-start.1 = ((bf16[128,16,128]{2,1,0:T(8,128)(2,1)}), bf16[128,16,128]{2,1,0:T(8,128)(2,1)S(1)}, u32[]{:S(2)}, u32[]{:S(2)}) async-start(bf16[128,16,128]{2,1,0:T(8,128)(2,1)} %get-tuple-element.29), calls=%async_computation.1 | async-start | bytes 1048576 | tf_op jit(solution)/shard_map/all_to_all | solution.py:457
  87.0 0.8 copy-start

commit v2 on v1

v2 whole, which is shorter than its diff:
```python
import math

import jax
import jax.numpy as jnp
from jax import lax
from jax.experimental import pallas as pl
from jax.experimental.pallas import tpu as pltpu
from jax.sharding import PartitionSpec as P

BF = jnp.bfloat16
F32 = jnp.float32
I32 = jnp.int32
AXES = ("gx", "gy")
INTERPRET = False
ROOT_2_PI = math.sqrt(2.0 / math.pi)


def dot_nn(a, b):
    return lax.dot_general(a, b, (((1,), (0,)), ((), ())), preferred_element_type=F32)


def dot_nt(a, b):
    return lax.dot_general(a, b, (((1,), (1,)), ((), ())), preferred_element_type=F32)


def iota(shape, dim):
    return lax.broadcasted_iota(I32, shape, dim)


def ones_where(mask):
    return jnp.where(mask, 1.0, 0.0).astype(BF)


def split(x):
    high = x.astype(BF)
    return high, (x - high.astype(F32)).astype(BF)


def pack_kernel(fields_ref, wells_ref, out_ref):
    row = iota((320, 1), 0)
    b = (row * 205) >> 13
    rho = row - 40 * b
    group = jnp.where(rho >= 20, 1, 0)
    t = rho - 20 * group
    y = 16 * b - 2 + t
    target = jnp.where((y >= 0) & (y < 128), group * 128 + y, -1)
    windows = ones_where(iota((320, 256), 1) == target)
    empty = jnp.zeros((128, 128), BF)

    def plane(j):
        return jnp.concatenate([fields_ref[j], fields_ref[10 + j] if j < 6 else empty], axis=1)

    lined = jnp.concatenate(
        [
            dot_nt(windows, jnp.concatenate([plane(2 * j), plane(2 * j + 1)], axis=0)).astype(BF)
            for j in range(5)
        ],
        axis=1,
    )
    channel, lane = iota((64, 128), 0), iota((64, 128), 1)
    wells = wells_ref[...]
    placed = jnp.concatenate(
        [
            dot_nn(wells, ones_where((channel >= 56) & (lane == channel + 64))),
            dot_nn(wells, ones_where((channel < 56) & (lane == channel + 72))),
        ],
        axis=0,
    ).astype(BF)
    target = jnp.where(t < 16, 16 * group + t, -1)
    extra = dot_nn(ones_where(iota((320, 32), 1) == target), placed)
    extra = jnp.concatenate([extra] * 4, axis=1)
    for part in range(4):
        lane = iota((1, 512), 1)
        within = lane & 127
        which = (within * 171) >> 11
        x = (lane >> 7) * 8 + 32 * part - 2 + within - 12 * which
        target = jnp.where((which < 10) & (x >= 0) & (x < 128), which * 128 + x, -1)
        spread = ones_where(iota((1280, 512), 0) == target)
        blocks = (dot_nn(lined, spread) + extra).astype(BF)
        for a in range(4):
            out_ref[4 * part + a] = blocks[:, 128 * a : 128 * a + 128].reshape(8, 40, 128)


def prep_kernel(
    well_ref,
    cell_ref,
    table_ref,
    lift_ref,
    down_ref,
    field_ref,
    cells_ref,
    rows_ref,
    half_ref,
    owner_ref,
    lanes_ref,
    big_ref,
    taps_ref,
    grad_ref,
):
    well = well_ref[...]
    used = well >= 0
    cells_ref[...] = ones_where(iota((4096, 256), 0) == jnp.where(used, cell_ref[...], -1))
    matches = ones_where(iota((2048, 256), 0) == well)
    table = table_ref[...]
    row = iota((8, 2048), 0)
    digits = jnp.where(row == 0, table >> 4, jnp.where(row == 1, table & 15, 0))
    found = dot_nn(digits.astype(F32).astype(BF), matches)
    slot = jnp.where(used, (found[0:1] * 16.0 + found[1:2]).astype(I32), -1)
    for half in range(2):
        place = jnp.where(
            used & (((slot >> 3) & 1) == half), (slot >> 4) * 8 + (slot & 7), -1
        )
        owner_ref[:, 256 * half : 256 * half + 256] = ones_where(iota((1024, 256), 0) == place)
    column = jnp.transpose(jnp.broadcast_to(slot, (128, 256)).astype(F32))[:, 0:1].astype(I32)
    place = jnp.where(column >= 0, ((column & 15) >> 1) * 128 + (column >> 4), -1)
    rows_ref[...] = ones_where(iota((256, 1024), 1) == place)
    half_ref[...] = jnp.where((iota((256, 512), 1) >> 8) == (column & 1), 1.0, 0.0)

    lane = iota((1, 640), 1)
    plane = lane & 15
    group = jnp.where(plane >= 10, 1, 0)
    target = (
        ((lane >> 4) & 1) * 256
        + group * 128
        + (plane - 10 * group) * 12
        + 2 * (lane >> 7)
        + ((lane >> 5) & 3)
    )
    lanes_ref[...] = ones_where(iota((512, 640), 0) == target)

    row = iota((512, 1), 0)
    x = (row >> 5) & 3
    y = 2 * ((row >> 7) & 1) + ((row >> 4) & 1)
    z = 2 * (row >> 8) + (row & 1)
    channel = (row >> 1) & 7
    col = iota((512, 256), 1)
    for px in range(2):
        for py in range(2):
            parts = []
            for pz in range(2):
                i, j, k = x - px, y - py, z - pz
                good = (i >= 0) & (i < 3) & (j >= 0) & (j < 3) & (k >= 0) & (k < 3)
                tap = jnp.where(good, ((i * 3 + j) * 3 + k) * 8 + channel, -1)
                parts.append(ones_where(col == tap))
            block = dot_nn(jnp.concatenate(parts, axis=1), lift_ref[...])
            at = (px * 2 + py) * 128
            big_ref[:, at : at + 128] = (0.5 * block).astype(BF)

    eye = ones_where(iota((64, 64), 0) == iota((64, 64), 1))
    turned = dot_nt(eye, down_ref[...]).astype(BF)
    for a in range(2):
        for b in range(2):
            for d in range(2):
                for p in range(4):
                    at = ((2 * a + p // 2) * 4 + 2 * b + p % 2) * 256 + d * 128
                    taps_ref[2 * a + b, 64 * d : 64 * d + 64, 128 * p : 128 * p + 128] = turned[
                        :, at : at + 128
                    ]

    row, col = iota((256, 256), 0), iota((256, 256), 1)
    turn = ones_where(col == (row & 7) * 32 + (row >> 3))
    for g in range(8):
        part = dot_nn(turn, field_ref[8 * g : 8 * g + 8].reshape(256, 128))
        for uv in range(32):
            grad_ref[8 * g : 8 * g + 8, 128 * uv : 128 * uv + 128] = part[
                8 * uv : 8 * uv + 8
            ]


def lift_kernel(
    tile_ref,
    arrived_ref,
    weight_ref,
    bias_ref,
    cells_ref,
    rows_ref,
    half_ref,
    lanes_ref,
    big_ref,
    grad_ref,
    send_ref,
    pairs_ref,
    last_ref,
    sorted_ref,
    shallow_ref,
    deep_ref,
    end_ref,
    even_ref,
    odd_ref,
    cot_ref,
    sum_ref,
):
    a, b = tile_ref[0], tile_ref[1]

    row, col = iota((256, 256), 0), iota((256, 256), 1)
    turn = ones_where(col == (row & 31) * 8 + (row >> 5))
    for tile in range(5):
        for pair in range(2):
            block = jnp.concatenate(
                [
                    arrived_ref[32 * s : 32 * s + 32, 8 * tile : 8 * tile + 8].reshape(256, 128)
                    for s in (2 * pair, 2 * pair + 1)
                ],
                axis=1,
            )
            part = dot_nn(turn, block).astype(BF)
            for r in range(8):
                group, t = divmod(8 * tile + r, 20)
                lane = 128 * (2 * (t % 2) + group)
                for s in range(2):
                    at = 128 * (t // 2) + 32 * (2 * pair + s)
                    sorted_ref[at : at + 32, lane : lane + 128] = part[
                        32 * r : 32 * r + 32, 128 * s : 128 * s + 128
                    ]

    end_ref[...] = jnp.zeros((5, 16, 256), F32)
    first = iota((128, 640), 0) == 0
    for half in range(2):
        whole = dot_nn(sorted_ref[640 * half : 640 * half + 640, :], lanes_ref[...])
        for r in range(5):
            y2 = 5 * half + r
            part = whole[128 * r : 128 * r + 128]
            moved = jnp.where(first, 0.0, pltpu.roll(part, 1, 0)).astype(BF)
            now = part.astype(BF)
            for u in range(5):
                lane = 128 * u
                deep_ref[u, 128 * y2 : 128 * y2 + 128, :] = now[:, lane : lane + 128]
                shallow_ref[u, 128 * y2 : 128 * y2 + 128, :] = moved[:, lane : lane + 128]
                if y2 < 9:
                    end_ref[u, y2 : y2 + 1, 0:128] = part[127:128, lane : lane + 128]
                if y2 > 0:
                    end_ref[u, y2 - 1 : y2, 128:256] = part[127:128, lane : lane + 128]

    lane, channel = iota((64, 512), 1) & 255, iota((64, 512), 0)
    fold = ones_where(lane == jnp.where(channel < 56, channel + 200, channel + 64))
    pulled = (dot_nn(rows_ref[...], sorted_ref[0:1024, :]) * half_ref[...]).astype(BF)
    spread = dot_nt(fold, pulled) * weight_ref[...]
    added = dot_nt(jnp.concatenate(split(spread), axis=0), cells_ref[...])
    grown = (grad_ref[...] + added[0:64] + added[64:128]).astype(BF)
    cot_ref[0:64, :] = grown
    lane = iota((64, 128), 1)
    ends = jnp.zeros((64, 128), F32)
    for uv in range(32):
        piece = grown[:, 128 * uv : 128 * uv + 128].astype(F32)
        moved = pltpu.roll(piece, 1, 1)
        cot_ref[64:128, 128 * uv : 128 * uv + 128] = jnp.where(lane == 0, 0.0, moved).astype(BF)
        at = (uv // 8) * 16 + uv % 8
        ends = jnp.where(lane == at, pltpu.roll(piece, at + 1, 1), ends)

    bias = bias_ref[...]

    def active(h):
        h = h + bias
        return h + h * jnp.tanh(h * (2.0 * ROOT_2_PI + (8.0 * 0.044715 * ROOT_2_PI) * (h * h)))

    lane = iota((16, 512), 1)
    start = jnp.where((iota((16, 512), 0) == 0) & (((lane >> 6) & 1) == 0), 0.0, 1.0)

    def multiply(n, out_ref):
        u = n // 3
        v = 3 * (n - 3 * u)
        near = pl.ds(pl.multiple_of(128 * v, 128), 384)
        far = pl.ds(pl.multiple_of(128 * v + 128, 128), 384)
        both = jnp.concatenate(
            [shallow_ref[u, near], shallow_ref[u, far], deep_ref[u, near], deep_ref[u, far]], axis=1
        )
        out_ref[...] = dot_nn(both, big_ref[...])

    def activate(n, in_ref):
        u = n // 3
        v = 3 * (n - 3 * u)
        for t in range(3):
            value = active(in_ref[128 * t : 128 * t + 128, :])
            pairs_ref[u, v + t] = value.astype(BF)
            pairs_ref[u, v + t, 0:16, :] = (value[0:16] * start).astype(BF)

    multiply(0, even_ref)

    def strips(n, carry):
        multiply(2 * n + 1, odd_ref)
        activate(2 * n, even_ref)
        multiply(2 * n + 2, even_ref)
        activate(2 * n + 1, odd_ref)
        return carry

    lax.fori_loop(0, 7, strips, 0)
    activate(14, even_ref)

    def clear(where, u, v, low):
        @pl.when(where)
        def _():
            for lane in low:
                shape = (5 if u is None else 1, 9 if v is None else 1, 128, 128)
                pairs_ref[
                    slice(None) if u is None else slice(u, u + 1),
                    slice(None) if v is None else slice(v, v + 1),
                    :,
                    lane : lane + 128,
                ] = jnp.zeros(shape, BF)

    clear(a == 0, 0, None, (0, 128))
    clear(a == 15, 4, None, (256, 384))
    clear(b == 0, None, 0, (0, 256))
    clear(b == 7, None, 8, (128, 384))

    row, lane = iota((80, 512), 0), iota((80, 512), 1)
    px, py, pz = lane >> 8, (lane >> 7) & 1, (lane >> 6) & 1
    u, v = row >> 4, row & 15
    keep = (
        (pz == 0)
        & (v < 9)
        & ~((a == 0) & (u == 0) & (px == 0))
        & ~((a == 15) & (u == 4) & (px == 1))
        & ~((b == 0) & (v == 0) & (py == 0))
        & ~((b == 7) & (v == 8) & (py == 1))
    )
    ending = active(dot_nn(end_ref[...].reshape(80, 256).astype(BF), big_ref[0:256, :]))
    ending = jnp.where(keep, ending, 0.0)
    last = jnp.concatenate([ending, jnp.zeros((48, 512), F32)], axis=0).astype(BF)
    last_ref[...] = last

    none = jnp.zeros((128, 128), BF)
    edges = []
    for shift in (0, 1, 16, 17):
        edge = pltpu.roll(ends, shift, 1) if shift else ends
        edges += [none[0:64], edge.astype(BF)]
    sum_ref[...] = dot_nn(jnp.concatenate(edges, axis=0), last)
    for u in range(5):
        sides = [i for i in range(2) if 0 <= u - i < 4]
        rows = []
        for i in sides:
            cot = cot_ref[:, 1024 * (u - i) : 1024 * (u - i) + 1024]
            rows += [
                jnp.concatenate([cot, none], axis=1),
                jnp.concatenate([none, cot], axis=1),
            ]
        at = 256 * sides[0]
        sum_ref[at : at + 128 * len(rows), :] += dot_nn(
            jnp.concatenate(rows, axis=0), pairs_ref[u].reshape(1152, 512)
        )
    for r in range(32):
        for j in range(4):
            send_ref[4 * r + j] = sum_ref[16 * r : 16 * r + 16, 128 * j : 128 * j + 128].astype(BF)


def coarse_kernel(
    pairs_ref,
    last_ref,
    taps_ref,
    bias_ref,
    weight_ref,
    cells_ref,
    owner_ref,
    coarse_ref,
    feat_ref,
    wide_ref,
):
    lane = iota((64, 128), 1)
    edge = jnp.zeros((64, 128), F32)
    for i in range(2):
        for j in range(2):
            part = dot_nt(taps_ref[2 * i + j, 64:128, :], last_ref[...])
            shift = (128 - 16 * i - j) % 128
            edge = edge + (pltpu.roll(part, shift, 1) if shift else part)
    bias = bias_ref[...]

    def layer(u, carry):
        total = None
        for i in range(2):
            for j in range(2):
                group = pairs_ref[u + i, j : j + 8].reshape(1024, 512)
                part = dot_nt(taps_ref[2 * i + j], group)
                total = part if total is None else total + part
        for v in range(8):
            near = total[0:64, 128 * v : 128 * v + 128]
            deep = pltpu.roll(total[64:128, 128 * v : 128 * v + 128], 127, 1)
            end = pltpu.roll(edge, 127 - (16 * u + v), 1)
            value = near + jnp.where(lane == 127, end, deep) + bias
            at = pl.multiple_of(1024 * u + 128 * v, 128)
            wide_ref[:, pl.ds(at, 128)] = value
        return carry

    lax.fori_loop(0, 4, layer, 0)

    picked = dot_nn(wide_ref[...].astype(BF), cells_ref[...]) * weight_ref[...]
    feat = jnp.zeros((1024, 128), F32)
    none = jnp.zeros((64, 256), BF)
    for part in split(picked):
        twice = jnp.concatenate(
            [jnp.concatenate([part, none], axis=1), jnp.concatenate([none, part], axis=1)], axis=0
        )
        feat = feat + dot_nt(owner_ref[...], twice)
    feat_ref[...] = feat.astype(BF).reshape(128, 8, 128)

    row, col = iota((256, 256), 0), iota((256, 256), 1)
    turn = ones_where(col == (row & 31) * 8 + (row >> 5))
    for g in range(8):
        tall = jnp.concatenate(
            [wide_ref[8 * g : 8 * g + 8, 128 * uv : 128 * uv + 128] for uv in range(32)], axis=0
        )
        part = dot_nn(turn, tall.astype(BF)).astype(BF)
        coarse_ref[8 * g : 8 * g + 8] = part.reshape(8, 32, 128)


def sum_kernel(scale, parts_ref, feat_ref, out_ref):
    total = jnp.sum(parts_ref[...].astype(F32), axis=0) * scale
    out_ref[:, 0:16, :] = jnp.broadcast_to(total.astype(BF)[None], (128, 16, 128))
    out_ref[:, 16:24, :] = feat_ref[...]


def finish_kernel(arrived_ref, grad_ref, feat_ref):
    eye = ones_where(iota((128, 128), 0) == iota((128, 128), 1))
    for a in range(2):
        for b in range(2):
            for d in range(2):
                base = 4 * (4 * a + 2 * b + d)
                for p in range(4):
                    block = jnp.concatenate(
                        [arrived_ref[4 * (base + t) + p, 0:16, :] for t in range(4)], axis=0
                    )
                    tap = ((2 * a + p // 2) * 4 + 2 * b + p % 2) * 4 + 2 * d
                    grad_ref[64 * tap : 64 * tap + 128, :] = dot_nt(eye, block)
    feat = jnp.sum(arrived_ref[:, 16:24, :].astype(F32), axis=0)
    feat_ref[0:8, :] = feat[:, 0:64]
    feat_ref[8:16, :] = pltpu.roll(feat, 64, 1)[:, 0:64]


def call(kernel, outs, scratch=(), scalars=0, cost=0):
    extra = {}
    if scalars:
        extra["in_specs"] = [pl.BlockSpec(memory_space=pltpu.SMEM)] + [
            pl.BlockSpec(memory_space=pltpu.VMEM)
        ] * scalars
    return pl.pallas_call(
        kernel,
        out_shape=[jax.ShapeDtypeStruct(shape, dtype) for shape, dtype in outs],
        scratch_shapes=[pltpu.VMEM(shape, dtype) for shape, dtype in scratch],
        compiler_params=pltpu.CompilerParams(vmem_limit_bytes=56 << 20),
        cost_estimate=pl.CostEstimate(flops=cost, bytes_accessed=1 << 20, transcendentals=0),
        interpret=INTERPRET,
        **extra,
    )


def pack(fields, well_grad):
    return call(pack_kernel, [((16, 8, 40, 128), BF)], cost=1 << 31)(
        fields.reshape(16, 128, 128), well_grad
    )[0].reshape(128, 40, 128)


def prepare(perf_well, perf_cell, well_slot, w_lift, down_weight, field_grad):
    flat = jnp.pad(w_lift.reshape(216, 64), ((0, 40), (0, 0)))
    none = jnp.zeros_like(flat)
    lift = jnp.concatenate(
        [jnp.concatenate([flat, none], axis=1), jnp.concatenate([none, flat], axis=1)], axis=0
    )
    outs = [
        ((4096, 256), BF),
        ((256, 1024), BF),
        ((256, 512), F32),
        ((1024, 512), BF),
        ((512, 640), BF),
        ((512, 512), BF),
        ((4, 128, 512), BF),
        ((64, 4096), F32),
    ]
    return call(prep_kernel, outs, cost=1 << 32)(
        perf_well,
        perf_cell,
        well_slot.reshape(1, 2048),
        lift,
        down_weight.reshape(4096, 64),
        field_grad.reshape(64, 32, 128),
    )


def lift(tile, arrived, perf_weight, b_lift, cells, rows, half, lanes, big, grad):
    outs = [((128, 16, 128), BF), ((5, 9, 128, 512), BF), ((128, 512), BF)]
    scratch = [
        ((1280, 512), BF),
        ((5, 1280, 128), BF),
        ((5, 1280, 128), BF),
        ((5, 16, 256), F32),
        ((384, 512), F32),
        ((384, 512), F32),
        ((128, 4096), BF),
        ((512, 512), F32),
    ]
    return call(lift_kernel, outs, scratch, scalars=9, cost=1 << 33)(
        tile,
        arrived,
        perf_weight,
        jnp.tile(0.5 * b_lift, 8)[None, :],
        cells,
        rows,
        half,
        lanes,
        big,
        grad,
    )


def coarsen(pairs, last, taps, b_down, perf_weight, cells, owner):
    outs = [((64, 32, 128), BF), ((128, 8, 128), BF)]
    return call(coarse_kernel, outs, [((64, 4096), F32)], cost=1 << 33)(
        pairs, last, taps, b_down[:, None], perf_weight, cells, owner
    )


def exchange(blocks):
    return lax.all_to_all(blocks, AXES, split_axis=0, concat_axis=0, tiled=True)


def body(
    fields,
    w_lift,
    b_lift,
    down_weight,
    b_down,
    perf_well,
    perf_cell,
    perf_weight,
    well_slot,
    well_grad,
    field_grad,
):
    scale = 1.0 / math.sqrt(64 * 64 * 128)
    tile = jnp.stack([lax.axis_index("gx"), lax.axis_index("gy")]).astype(I32)
    arrived = exchange(pack(fields, well_grad))
    cells, rows, half, owner, lanes, big, taps, grad = prepare(
        perf_well, perf_cell, well_slot, w_lift, down_weight, field_grad
    )
    parts, pairs, last = lift(
        tile, arrived, perf_weight, b_lift, cells, rows, half, lanes, big, grad
    )
    parts = exchange(parts)
    coarse, feat = coarsen(pairs, last, taps, b_down, perf_weight, cells, owner)
    shared = call(
        lambda *refs: sum_kernel(scale, *refs), [((128, 24, 128), BF)], cost=1 << 20
    )(parts, feat)[0]
    shared = exchange(shared)
    down_grad, well_feat = call(
        finish_kernel, [((4096, 64), F32), ((16, 64), F32)], cost=1 << 28
    )(shared)
    return (
        coarse.reshape(64, 4, 8, 128),
        well_feat,
        down_grad.reshape(4, 4, 4, 64, 64),
    )


def solution(mesh):
    placed = (
        P(None, AXES, None, None),
        P(),
        P(),
        P(),
        P(),
        P(AXES, None),
        P(AXES, None),
        P(AXES, None),
        P(),
        P(AXES, None),
        P(None, "gx", "gy", None),
    )
    return jax.shard_map(
        body,
        mesh=mesh,
        in_specs=placed,
        out_specs=(P(None, "gx", "gy", None), P(AXES, None), P()),
        check_vma=False,
    )
```

time: 119 us -> 106 us (0.89)
  Pallas kernels: 54.5 us -> 45.5 us
  waiting for transfers between devices: 16 us -> 13.7 us
  local copies, waits for them, and re-layouts: 4.81 us -> 3.29 us
    pallas_call x1, Pallas kernels: 25.4 us -> 16 us  [lift(): call(lift_kernel, outs, scratch, scalars=9, cost=1 << 33)]
    all_to_all x2, waiting for transfers between devices: 16 us -> 13.7 us  [exchange(): return lax.all_to_all(blocks, AXES, split_axis=0, concat_axis=0, tiled=True)]
  transfers between devices with their start and end apart: 2 -> 2, of which waited for: 2 -> 2; matrix products, arithmetic and copies ran while one was open for 2% -> 3% of each run, Pallas kernels for 17% -> 19%
where the time goes in v2:
time: 106 us
  Pallas kernels  45.5 us (43%)
  blocking collectives  25.8 us (24%)
  starting transfers between devices  15.4 us (15%)
  waiting for transfers between devices  13.7 us (13%)
  local copies, waits for them, and re-layouts  3.29 us (3%)
  other arithmetic  1.32 us (1%)
    all_to_all x1, blocking collectives, exchange(): return lax.all_to_all(blocks, AXES, split_axis=0, concat_axis=0, tiled=True)  25.8 us
    pallas_call x1, Pallas kernels, lift(): call(lift_kernel, outs, scratch, scalars=9, cost=1 << 33)  16 us
    all_to_all x2, starting transfers between devices, exchange(): return lax.all_to_all(blocks, AXES, split_axis=0, concat_axis=0, tiled=True)  15.4 us
    all_to_all x2, waiting for transfers between devices, exchange(): return lax.all_to_all(blocks, AXES, split_axis=0, concat_axis=0, tiled=True)  13.7 us
    pallas_call x1, Pallas kernels, coarsen(): call(coarse_kernel, outs, [((64, 4096), F32)], cost=1 << 33)  13.1 us
    pallas_call x1, Pallas kernels, prepare(): call(prep_kernel, outs, cost=1 << 32)  6.87 us
    pallas_call x1, Pallas kernels, pack(): call(pack_kernel, [((16, 8, 40, 128), BF)], cost=1 << 31)  4.43 us
    pallas_call x1, Pallas kernels, body(): call(finish_kernel, [((4096, 64), F32), ((16, 64), F32)], cost=1 << 28)  2.87 us
  transfers between devices with their start and end apart: 2, of which 2 were waited for; matrix products, arithmetic and copies ran while one was open for 3% of the time, Pallas kernels for 19%

profile of v2, /device:TPU:1, one launch (start us, length us, event | category | flops | bytes accessed | tf_op | source)
XLA Modules:
  0.0 105.6 jit_solution(17568571608297794212)
XLA Ops:
  0.6 4.4 %shard_map.130 = bf16[16,8,40,128]{3,2,1,0:T(8,128)(2,1)} custom-call(bf16[16,128,128]{2,1,0:T(8,128)(2,1)} %bitcast.15, bf16[16,64]{1,0:T(8,128)(2,1)} %wells_ref.1), custom_call_target="tpu_custom_call" | custom-call | flops 2147483648 | bytes 1048576 | tf_op jit(solution)/shard_map/pallas_call | solution.py:446
  5.1 0.0 copy-start.4
  5.1 0.0 copy-start.3
  5.1 0.0 copy-start.2
  5.1 11.5 %all-to-all-start = ((bf16[128,40,128]{2,1,0:T(8,128)(2,1)}), bf16[128,40,128]{2,1,0:T(8,128)(2,1)S(1)}, u32[]{:S(2)}, u32[]{:S(2)}) async-start(bf16[128,40,128]{2,1,0:T(8,128)(2,1)} %bitcast.11), calls=%async_computation | async-start | bytes 2621440 | tf_op jit(solution)/shard_map/all_to_all | solution.py:511
  16.6 0.0 copy-done.4
  16.6 0.7 broadcast_in_dim_tile.3.bias_ref
  17.3 0.0 copy-done.3
  17.3 0.7 copy.14.bias_ref
  17.9 0.0 copy-done.2
  18.0 0.6 pad_add_fusion.tile_ref
  18.6 0.7 fusion.2.lift_ref
  19.3 6.9 %shard_map.131 = (bf16[4096,256]{1,0:T(8,128)(2,1)}, bf16[256,1024]{1,0:T(8,128)(2,1)}, f32[256,512]{1,0:T(8,128)}, bf16[1024,512]{1,0:T(8,128)(2,1)}, bf16[512,...) custom-call(s32[1,256]{1,0:T(1,128)} %well_ref.1, ...), custom_call_target="tpu_custom_call" | custom-call | flops 4294967296 | bytes 1048576 | tf_op jit(solution)/shard_map/pallas_call | solution.py:467
  26.2 12.7 %all-to-all-done.arrived_ref = bf16[128,40,128]{2,1,0:T(8,128)(2,1)S(1)} async-done(((bf16[128,40,128]{2,1,0:T(8,128)(2,1)}), bf16[128,40,128]{2,1,0:T(8,128)(2,1)S(1)}, u32[]{:S(2)}, u32[]{:S(2)}) %all-to-all-start) | async-done | bytes 1310752 | tf_op jit(solution)/shard_map/all_to_all | solution.py:511
  38.9 0.0 copy-start.1
  38.9 1.1 %copy-done.1 = bf16[128,40,128]{2,1,0:T(8,128)(2,1)} copy-done((bf16[128,40,128]{2,1,0:T(8,128)(2,1)}, bf16[128,40,128]{2,1,0:T(8,128)(2,1)S(1)}, u32[]{:S(2)}) %copy-start.1) | copy-done | bytes 1310744
  40.0 16.0 %shard_map.132 = (bf16[128,16,128]{2,1,0:T(8,128)(2,1)}, bf16[5,9,128,512]{3,2,1,0:T(8,128)(2,1)}, bf16[128,512]{1,0:T(8,128)(2,1)}) custom-call(s32[2]{0:T(128)} %pad_add_fusion.tile_ref, bf16[128,40,128]{2,1,0:T(8,128)(2,1)} %copy-done.1, f32[1,256]{1,0:T(1,128)} %weight_ref.3, f32[1,512]{1,0:T(1,128)} %broadcast_in_dim_tile.3.bias_ref, ...), custom_call_target="tpu_custom_call" | custom-call | flops 8589934592 | bytes 1048576 | tf_op jit(solution)/shard_map/pallas_call | solution.py:489
  56.0 3.9 %all-to-all-start.1 = ((bf16[128,16,128]{2,1,0:T(8,128)(2,1)}), bf16[128,16,128]{2,1,0:T(8,128)(2,1)S(1)}, u32[]{:S(2)}, u32[]{:S(2)}) async-start(bf16[128,16,128]{2,1,0:T(8,128)(2,1)} %get-tuple-element.29), calls=%async_computation.1 | async-start | bytes 1048576 | tf_op jit(solution)/shard_map/all_to_all | solution.py:511
  59.9 13.1 %shard_map.133 = (bf16[64,32,128]{2,1,0:T(8,128)(2,1)}, bf16[128,8,128]{2,1,0:T(8,128)(2,1)}) custom-call(bf16[5,9,128,512]{3,2,1,0:T(8,128)(2,1)} %get-tuple-element.24.pairs_ref, bf16[128,512]{1,0:T(8,128)(2,1)} %get-tuple-element.25.last_ref, bf16[4,128,512]{2,1,0:T(8,128)(2,1)} %get-tuple-element.26.taps_ref, f32[64,1]{1,0:T(8,128)} %copy.14.bias_ref, ...), custom_call_target="tpu_custom_call" | custom-call | flops 8589934592 | bytes 1048576 | tf_op jit(solution)/shard_map/pallas_call | solution.py:505
  73.0 0.9 all-to-all-done.1.refs_0_
  73.9 0.8 copy-done
  74.7 2.2 %shard_map.134 = bf16[128,24,128]{2,1,0:T(8,128)(2,1)} custom-call(bf16[128,16,128]{2,1,0:T(8,128)(2,1)} %copy-done, bf16[128,8,128]{2,1,0:T(8,128)(2,1)} %get-tuple-element.30.refs_1_), custom_call_target="tpu_custom_call" | custom-call | flops 1048576 | bytes 1048576 | tf_op jit(solution)/shard_map/pallas_call | solution.py:538
  76.9 25.8 %all_to_all.15.arrived_ref = bf16[128,24,128]{2,1,0:T(8,128)(2,1)} all-to-all(bf16[128,24,128]{2,1,0:T(8,128)(2,1)} %shard_map.134), channel_id=1, replica_groups=mesh['gx'=16,'gy'=8] {'gx','gy'}, dimensions={0} | all-to-all | bytes 1572864 | tf_op jit(solution)/shard_map/all_to_all | solution.py:511
  102.7 2.9 %shard_map.135 = (f32[4096,64]{1,0:T(8,128)}, f32[16,64]{1,0:T(8,128)}) custom-call(bf16[128,24,128]{2,1,0:T(8,128)(2,1)} %all_to_all.15.arrived_ref), custom_call_target="tpu_custom_call" | custom-call | flops 268435456 | bytes 1048576 | tf_op jit(solution)/shard_map/pallas_call | solution.py:542
  (4 shorter events, 0.0 us)
Async XLA Ops:
  5.1 11.5 %copy-start.4 = (f32[64]{0:T(128)S(1)}, f32[64]{0:T(128)}, u32[]{:S(2)}) copy-start(f32[64]{0:T(128)} %param.13) | copy-start | bytes 772
  5.1 12.2 %copy-start.3 = (f32[64]{0:T(128)S(1)}, f32[64]{0:T(128)}, u32[]{:S(2)}) copy-start(f32[64]{0:T(128)} %param.15) | copy-start | bytes 772
  5.1 12.9 %copy-start.2 = (bf16[3,3,3,8,64]{4,3,2,1,0:T(8,128)(2,1)S(1)}, bf16[3,3,3,8,64]{4,3,2,1,0:T(8,128)(2,1)}, u32[]{:S(2)}) copy-start(bf16[3,3,3,8,64]{4,3,2,1,0:T(8,128)(2,1)} %param.12) | copy-start | bytes 82948
  5.1 33.8 %all-to-all-start = ((bf16[128,40,128]{2,1,0:T(8,128)(2,1)}), bf16[128,40,128]{2,1,0:T(8,128)(2,1)S(1)}, u32[]{:S(2)}, u32[]{:S(2)}) async-start(bf16[128,40,128]{2,1,0:T(8,128)(2,1)} %bitcast.11), calls=%async_computation | async-start | bytes 2621440 | tf_op jit(solution)/shard_map/all_to_all | solution.py:511
  38.9 1.1 %copy-start.1 = (bf16[128,40,128]{2,1,0:T(8,128)(2,1)}, bf16[128,40,128]{2,1,0:T(8,128)(2,1)S(1)}, u32[]{:S(2)}) copy-start(bf16[128,40,128]{2,1,0:T(8,128)(2,1)S(1)} %all-to-all-done.arrived_ref) | copy-start | bytes 3932164
  56.0 17.9 %all-to-all-start.1 = ((bf16[128,16,128]{2,1,0:T(8,128)(2,1)}), bf16[128,16,128]{2,1,0:T(8,128)(2,1)S(1)}, u32[]{:S(2)}, u32[]{:S(2)}) async-start(bf16[128,16,128]{2,1,0:T(8,128)(2,1)} %get-tuple-element.29), calls=%async_computation.1 | async-start | bytes 1048576 | tf_op jit(solution)/shard_map/all_to_all | solution.py:511
  73.9 0.8 copy-start

commit v3 on v2

--- a/solution.py
+++ b/solution.py
@@ -12,6 +12,7 @@
 I32 = jnp.int32
 AXES = ("gx", "gy")
 INTERPRET = False
+ROOM_LIFT = 58
 ROOT_2_PI = math.sqrt(2.0 / math.pi)
 
 
@@ -146,16 +147,15 @@
             at = (px * 2 + py) * 128
             big_ref[:, at : at + 128] = (0.5 * block).astype(BF)
 
-    eye = ones_where(iota((64, 64), 0) == iota((64, 64), 1))
-    turned = dot_nt(eye, down_ref[...]).astype(BF)
     for a in range(2):
         for b in range(2):
-            for d in range(2):
-                for p in range(4):
-                    at = ((2 * a + p // 2) * 4 + 2 * b + p % 2) * 256 + d * 128
-                    taps_ref[2 * a + b, 64 * d : 64 * d + 64, 128 * p : 128 * p + 128] = turned[
-                        :, at : at + 128
-                    ]
+            for p in range(4):
+                at = ((2 * a + p // 2) * 4 + 2 * b + p % 2) * 256
+                taps_ref[
+                    128 * p : 128 * p + 128, 128 * (2 * a + b) : 128 * (2 * a + b) + 128
+                ] = jnp.concatenate(
+                    [down_ref[at : at + 128, :], down_ref[at + 128 : at + 256, :]], axis=1
+                )
 
     row, col = iota((256, 256), 0), iota((256, 256), 1)
     turn = ones_where(col == (row & 7) * 32 + (row >> 3))
@@ -172,15 +172,15 @@
     arrived_ref,
     weight_ref,
     bias_ref,
-    cells_ref,
-    rows_ref,
-    half_ref,
     lanes_ref,
-    big_ref,
-    grad_ref,
+    cells_far,
+    rows_far,
+    half_far,
+    big_far,
+    grad_far,
     send_ref,
-    pairs_ref,
     last_ref,
+    pairs_far,
     sorted_ref,
     shallow_ref,
     deep_ref,
@@ -189,8 +189,30 @@
     odd_ref,
     cot_ref,
     sum_ref,
+    pairs_ref,
+    cells_ref,
+    rows_ref,
+    half_ref,
+    big_ref,
+    grad_ref,
+    arrive,
+    leave,
 ):
     a, b = tile_ref[0], tile_ref[1]
+    fetch = [
+        pltpu.make_async_copy(source, target, arrive.at[n])
+        for n, (source, target) in enumerate(
+            [
+                (rows_far, rows_ref),
+                (half_far, half_ref),
+                (cells_far, cells_ref),
+                (grad_far, grad_ref),
+                (big_far, big_ref),
+            ]
+        )
+    ]
+    for copy in fetch:
+        copy.start()
 
     row, col = iota((256, 256), 0), iota((256, 256), 1)
     turn = ones_where(col == (row & 31) * 8 + (row >> 5))
@@ -231,6 +253,8 @@
                 if y2 > 0:
                     end_ref[u, y2 - 1 : y2, 128:256] = part[127:128, lane : lane + 128]
 
+    for copy in fetch:
+        copy.wait()
     lane, channel = iota((64, 512), 1) & 255, iota((64, 512), 0)
     fold = ones_where(lane == jnp.where(channel < 56, channel + 200, channel + 64))
     pulled = (dot_nn(rows_ref[...], sorted_ref[0:1024, :]) * half_ref[...]).astype(BF)
@@ -302,6 +326,12 @@
     clear(a == 15, 4, None, (256, 384))
     clear(b == 0, None, 0, (0, 256))
     clear(b == 7, None, 8, (128, 384))
+
+    stores = [
+        pltpu.make_async_copy(pairs_ref.at[u], pairs_far.at[u], leave.at[u]) for u in range(5)
+    ]
+    for copy in stores:
+        copy.start()
 
     row, lane = iota((80, 512), 0), iota((80, 512), 1)
     px, py, pz = lane >> 8, (lane >> 7) & 1, (lane >> 6) & 1
@@ -341,47 +371,68 @@
     for r in range(32):
         for j in range(4):
             send_ref[4 * r + j] = sum_ref[16 * r : 16 * r + 16, 128 * j : 128 * j + 128].astype(BF)
+    for copy in stores:
+        copy.wait()
 
 
 def coarse_kernel(
-    pairs_ref,
+    taps_ref,
     last_ref,
-    taps_ref,
     bias_ref,
     weight_ref,
-    cells_ref,
-    owner_ref,
+    pairs_far,
+    cells_far,
+    owner_far,
     coarse_ref,
     feat_ref,
     wide_ref,
+    tall_ref,
+    first_ref,
+    second_ref,
+    third_ref,
+    pairs_ref,
+    cells_ref,
+    owner_ref,
+    arrive,
 ):
-    lane = iota((64, 128), 1)
-    edge = jnp.zeros((64, 128), F32)
-    for i in range(2):
-        for j in range(2):
-            part = dot_nt(taps_ref[2 * i + j, 64:128, :], last_ref[...])
-            shift = (128 - 16 * i - j) % 128
-            edge = edge + (pltpu.roll(part, shift, 1) if shift else part)
+    fetch = [
+        pltpu.make_async_copy(pairs_far.at[u], pairs_ref.at[u], arrive.at[u]) for u in range(5)
+    ]
+    fetch += [
+        pltpu.make_async_copy(cells_far, cells_ref, arrive.at[5]),
+        pltpu.make_async_copy(owner_far, owner_ref, arrive.at[6]),
+    ]
+    for copy in fetch:
+        copy.start()
+
+    edges = dot_nn(last_ref[...], taps_ref[...])
+    edge = edges[:, 0:128]
+    for n, shift in enumerate((127, 112, 111)):
+        edge = edge + pltpu.roll(edges[:, 128 * n + 128 : 128 * n + 256], shift, 0)
     bias = bias_ref[...]
-
-    def layer(u, carry):
-        total = None
-        for i in range(2):
-            for j in range(2):
-                group = pairs_ref[u + i, j : j + 8].reshape(1024, 512)
-                part = dot_nt(taps_ref[2 * i + j], group)
-                total = part if total is None else total + part
+    bottom = iota((128, 128), 0) == 127
+    slots = (first_ref, second_ref, third_ref)
+    for u in range(5):
+        fetch[u].wait()
+        slots[u % 3][...] = dot_nn(pairs_ref[u].reshape(1152, 512), taps_ref[...])
+        if u == 0:
+            continue
+        near, far = slots[(u - 1) % 3], slots[u % 3]
         for v in range(8):
-            near = total[0:64, 128 * v : 128 * v + 128]
-            deep = pltpu.roll(total[64:128, 128 * v : 128 * v + 128], 127, 1)
-            end = pltpu.roll(edge, 127 - (16 * u + v), 1)
-            value = near + jnp.where(lane == 127, end, deep) + bias
-            at = pl.multiple_of(1024 * u + 128 * v, 128)
-            wide_ref[:, pl.ds(at, 128)] = value
-        return carry
-
-    lax.fori_loop(0, 4, layer, 0)
-
+            at = 128 * v
+            total = (near[at : at + 128, 0:128] + near[at + 128 : at + 256, 128:256]) + (
+                far[at : at + 128, 256:384] + far[at + 128 : at + 256, 384:512]
+            )
+            row = 16 * (u - 1) + v
+            deep = jnp.where(bottom, edge[row : row + 1], pltpu.roll(total, 127, 0))
+            value = total + pltpu.roll(deep, 64, 1) + bias
+            at = 1024 * (u - 1) + 128 * v
+            tall_ref[at : at + 128, :] = value.astype(BF)
+
+    eye = ones_where(iota((64, 128), 0) == iota((64, 128), 1))
+    wide_ref[...] = dot_nt(eye, tall_ref[...])
+    fetch[5].wait()
+    fetch[6].wait()
     picked = dot_nn(wide_ref[...].astype(BF), cells_ref[...]) * weight_ref[...]
     feat = jnp.zeros((1024, 128), F32)
     none = jnp.zeros((64, 256), BF)
@@ -425,17 +476,20 @@
     feat_ref[8:16, :] = pltpu.roll(feat, 64, 1)[:, 0:64]
 
 
-def call(kernel, outs, scratch=(), scalars=0, cost=0):
+VMEM, SMEM, HBM = pltpu.VMEM, pltpu.SMEM, pltpu.HBM
+
+
+def call(kernel, outs, scratch=(), spaces=None, semaphores=(), cost=0, room=56):
     extra = {}
-    if scalars:
-        extra["in_specs"] = [pl.BlockSpec(memory_space=pltpu.SMEM)] + [
-            pl.BlockSpec(memory_space=pltpu.VMEM)
-        ] * scalars
+    if spaces is not None:
+        places = [pl.BlockSpec(memory_space=space) for space in spaces]
+        extra = {"in_specs": places[: -len(outs)], "out_specs": places[-len(outs) :]}
     return pl.pallas_call(
         kernel,
         out_shape=[jax.ShapeDtypeStruct(shape, dtype) for shape, dtype in outs],
-        scratch_shapes=[pltpu.VMEM(shape, dtype) for shape, dtype in scratch],
-        compiler_params=pltpu.CompilerParams(vmem_limit_bytes=56 << 20),
+        scratch_shapes=[pltpu.VMEM(shape, dtype) for shape, dtype in scratch]
+        + [pltpu.SemaphoreType.DMA((count,)) for count in semaphores],
+        compiler_params=pltpu.CompilerParams(vmem_limit_bytes=room << 20),
         cost_estimate=pl.CostEstimate(flops=cost, bytes_accessed=1 << 20, transcendentals=0),
         interpret=INTERPRET,
         **extra,
@@ -461,7 +515,7 @@
         ((1024, 512), BF),
         ((512, 640), BF),
         ((512, 512), BF),
-        ((4, 128, 512), BF),
+        ((512, 512), BF),
         ((64, 4096), F32),
     ]
     return call(prep_kernel, outs, cost=1 << 32)(
@@ -475,7 +529,7 @@
 
 
 def lift(tile, arrived, perf_weight, b_lift, cells, rows, half, lanes, big, grad):
-    outs = [((128, 16, 128), BF), ((5, 9, 128, 512), BF), ((128, 512), BF)]
+    outs = [((128, 16, 128), BF), ((128, 512), BF), ((5, 9, 128, 512), BF)]
     scratch = [
         ((1280, 512), BF),
         ((5, 1280, 128), BF),
@@ -485,25 +539,36 @@
         ((384, 512), F32),
         ((128, 4096), BF),
         ((512, 512), F32),
+        ((5, 9, 128, 512), BF),
+        ((4096, 256), BF),
+        ((256, 1024), BF),
+        ((256, 512), F32),
+        ((512, 512), BF),
+        ((64, 4096), F32),
     ]
-    return call(lift_kernel, outs, scratch, scalars=9, cost=1 << 33)(
-        tile,
-        arrived,
-        perf_weight,
-        jnp.tile(0.5 * b_lift, 8)[None, :],
-        cells,
-        rows,
-        half,
-        lanes,
-        big,
-        grad,
+    spaces = [SMEM] + [VMEM] * 4 + [HBM] * 5 + [VMEM, VMEM, HBM]
+    bias = jnp.tile(0.5 * b_lift, 8)[None, :]
+    return call(lift_kernel, outs, scratch, spaces, (5, 5), cost=1 << 33, room=ROOM_LIFT)(
+        tile, arrived, perf_weight, bias, lanes, cells, rows, half, big, grad
     )
 
 
 def coarsen(pairs, last, taps, b_down, perf_weight, cells, owner):
     outs = [((64, 32, 128), BF), ((128, 8, 128), BF)]
-    return call(coarse_kernel, outs, [((64, 4096), F32)], cost=1 << 33)(
-        pairs, last, taps, b_down[:, None], perf_weight, cells, owner
+    scratch = [
+        ((64, 4096), F32),
+        ((4096, 128), BF),
+        ((1152, 512), F32),
+        ((1152, 512), F32),
+        ((1152, 512), F32),
+        ((5, 9, 128, 512), BF),
+        ((4096, 256), BF),
+        ((1024, 512), BF),
+    ]
+    spaces = [VMEM] * 4 + [HBM] * 3 + [VMEM] * 2
+    bias = jnp.tile(b_down, 2)[None, :]
+    return call(coarse_kernel, outs, scratch, spaces, (7,), cost=1 << 33)(
+        taps, last, bias, perf_weight, pairs, cells, owner
     )
 
 
@@ -530,17 +595,17 @@
     cells, rows, half, owner, lanes, big, taps, grad = prepare(
         perf_well, perf_cell, well_slot, w_lift, down_weight, field_grad
     )
-    parts, pairs, last = lift(
+    parts, last, pairs = lift(
         tile, arrived, perf_weight, b_lift, cells, rows, half, lanes, big, grad
     )
     parts = exchange(parts)
     coarse, feat = coarsen(pairs, last, taps, b_down, perf_weight, cells, owner)
     shared = call(
-        lambda *refs: sum_kernel(scale, *refs), [((128, 24, 128), BF)], cost=1 << 20
+        lambda *refs: sum_kernel(scale, *refs), [((128, 24, 128), BF)], cost=1 << 20, room=8
     )(parts, feat)[0]
     shared = exchange(shared)
     down_grad, well_feat = call(
-        finish_kernel, [((4096, 64), F32), ((16, 64), F32)], cost=1 << 28
+        finish_kernel, [((4096, 64), F32), ((16, 64), F32)], cost=1 << 28, room=8
     )(shared)
     return (
         coarse.reshape(64, 4, 8, 128),

time: 106 us -> 99.2 us (0.936)
  Pallas kernels: 45.5 us -> 39 us
  blocking collectives: 25.8 us -> 22.3 us
  waiting for transfers between devices: 13.7 us -> 16.7 us
    pallas_call x3, Pallas kernels: 32 us -> 27.3 us  [the longest x1 15.6 us: lift(): call(lift_kernel, outs, scratch, spaces, (5, 5), cost=1 << 33, room=ROOM_...]
    all_to_all x1, blocking collectives: 25.8 us -> 22.3 us  [exchange(): return lax.all_to_all(blocks, AXES, split_axis=0, concat_axis=0, tiled=True)]
    all_to_all x2, waiting for transfers between devices: 13.7 us -> 16.7 us  [exchange(): return lax.all_to_all(blocks, AXES, split_axis=0, concat_axis=0, tiled=True)]
    pallas_call x1, Pallas kernels: 2.18 us -> 0.19 us  [body(): call(lambda *refs: sum_kernel(scale, *refs), [((128, 24, 128), BF)], cost...]
  transfers between devices with their start and end apart: 2 -> 2, of which waited for: 2 -> 2; matrix products, arithmetic and copies ran while one was open for 3% -> 3% of each run, Pallas kernels for 19% -> 17%
where the time goes in v3:
time: 99.2 us; the launch traced here: 98.8 us
  Pallas kernels  39 us (39%)
  blocking collectives  22.3 us (22%)
  waiting for transfers between devices  16.7 us (17%)
  starting transfers between devices  15.4 us (16%)
  local copies, waits for them, and re-layouts  3.31 us (3%)
  other arithmetic  1.33 us (1%)
    all_to_all x1, blocking collectives, exchange(): return lax.all_to_all(blocks, AXES, split_axis=0, concat_axis=0, tiled=True)  22.3 us
    all_to_all x2, waiting for transfers between devices, exchange(): return lax.all_to_all(blocks, AXES, split_axis=0, concat_axis=0, tiled=True)  16.7 us
    pallas_call x1, Pallas kernels, lift(): call(lift_kernel, outs, scratch, spaces, (5, 5), cost=1 << 33, room=ROOM_...  15.6 us
    all_to_all x2, starting transfers between devices, exchange(): return lax.all_to_all(blocks, AXES, split_axis=0, concat_axis=0, tiled=True)  15.4 us
    pallas_call x1, Pallas kernels, coarsen(): call(coarse_kernel, outs, scratch, spaces, (7,), cost=1 << 33)  9.98 us
    pallas_call x1, Pallas kernels, prepare(): call(prep_kernel, outs, cost=1 << 32)  7.05 us
    pallas_call x1, Pallas kernels, pack(): call(pack_kernel, [((16, 8, 40, 128), BF)], cost=1 << 31)  4.43 us
    unnamed x10, local copies, waits for them, and re-layouts  2.07 us
  transfers between devices with their start and end apart: 2, of which 2 were waited for; matrix products, arithmetic and copies ran while one was open for 3% of the time, Pallas kernels for 17%

profile of v3, /device:TPU:1, one launch (start us, length us, event | category | flops | bytes accessed | tf_op | source)
XLA Modules:
  0.0 98.8 jit_solution(18195586216459648443)
XLA Ops:
  0.6 4.4 %shard_map.131 = bf16[16,8,40,128]{3,2,1,0:T(8,128)(2,1)} custom-call(bf16[16,128,128]{2,1,0:T(8,128)(2,1)} %bitcast.13, bf16[16,64]{1,0:T(8,128)(2,1)} %wells_ref.1), custom_call_target="tpu_custom_call" | custom-call | flops 2147483648 | bytes 1048576 | tf_op jit(solution)/shard_map/pallas_call | solution.py:500
  5.1 0.0 copy-start.3
  5.1 0.0 copy-start.4
  5.1 0.0 copy-start.2
  5.1 11.5 %all-to-all-start = ((bf16[128,40,128]{2,1,0:T(8,128)(2,1)}), bf16[128,40,128]{2,1,0:T(8,128)(2,1)S(1)}, u32[]{:S(2)}, u32[]{:S(2)}) async-start(bf16[128,40,128]{2,1,0:T(8,128)(2,1)} %bitcast.10), calls=%async_computation | async-start | bytes 2621440 | tf_op jit(solution)/shard_map/all_to_all | solution.py:576
  16.6 0.0 copy-done.3
  16.6 0.7 broadcast_in_dim_tile.6.bias_ref
  17.3 0.0 copy-done.4
  17.3 0.6 broadcast_in_dim_tile.7.bias_ref
  17.8 0.0 copy-done.2
  17.8 0.6 pad_add_fusion.tile_ref
  18.4 0.7 fusion.2.lift_ref
  19.2 7.0 %shard_map.130 = (bf16[4096,256]{1,0:T(8,128)(2,1)}, bf16[256,1024]{1,0:T(8,128)(2,1)}, f32[256,512]{1,0:T(8,128)}, bf16[1024,512]{1,0:T(8,128)(2,1)}, bf16[512,...) custom-call(s32[1,256]{1,0:T(1,128)} %well_ref.1, ...), custom_call_target="tpu_custom_call" | custom-call | flops 4294967296 | bytes 1048576 | tf_op jit(solution)/shard_map/pallas_call | solution.py:521
  26.2 12.7 %all-to-all-done.arrived_ref = bf16[128,40,128]{2,1,0:T(8,128)(2,1)S(1)} async-done(((bf16[128,40,128]{2,1,0:T(8,128)(2,1)}), bf16[128,40,128]{2,1,0:T(8,128)(2,1)S(1)}, u32[]{:S(2)}, u32[]{:S(2)}) %all-to-all-start) | async-done | bytes 1310752 | tf_op jit(solution)/shard_map/all_to_all | solution.py:576
  38.9 0.0 copy-start.1
  38.9 1.1 %copy-done.1 = bf16[128,40,128]{2,1,0:T(8,128)(2,1)} copy-done((bf16[128,40,128]{2,1,0:T(8,128)(2,1)}, bf16[128,40,128]{2,1,0:T(8,128)(2,1)S(1)}, u32[]{:S(2)}) %copy-start.1) | copy-done | bytes 1310744
  40.0 15.6 %shard_map.132 = (bf16[128,16,128]{2,1,0:T(8,128)(2,1)}, bf16[128,512]{1,0:T(8,128)(2,1)}, bf16[5,9,128,512]{3,2,1,0:T(8,128)(2,1)}) custom-call(s32[2]{0:T(128)} %pad_add_fusion.tile_ref, bf16[128,40,128]{2,1,0:T(8,128)(2,1)} %copy-done.1, f32[1,256]{1,0:T(1,128)} %weight_ref.3, f32[1,512]{1,0:T(1,128)} %broadcast_in_dim_tile.6.bias_ref, ...), custom_call_target="tpu_custom_call" | custom-call | flops 8589934592 | bytes 1048576 | tf_op jit(solution)/shard_map/pallas_call | solution.py:551
  55.7 3.9 %all-to-all-start.1 = ((bf16[128,16,128]{2,1,0:T(8,128)(2,1)}), bf16[128,16,128]{2,1,0:T(8,128)(2,1)S(1)}, u32[]{:S(2)}, u32[]{:S(2)}) async-start(bf16[128,16,128]{2,1,0:T(8,128)(2,1)} %get-tuple-element.29), calls=%async_computation.1 | async-start | bytes 1048576 | tf_op jit(solution)/shard_map/all_to_all | solution.py:576
  59.5 10.0 %shard_map.133 = (bf16[64,32,128]{2,1,0:T(8,128)(2,1)}, bf16[128,8,128]{2,1,0:T(8,128)(2,1)}) custom-call(bf16[512,512]{1,0:T(8,128)(2,1)} %get-tuple-element.18.taps_ref, bf16[128,512]{1,0:T(8,128)(2,1)} %get-tuple-element.25.last_ref, f32[1,128]{1,0:T(1,128)} %broadcast_in_dim_tile.7.bias_ref, f32[1,256]{1,0:T(1,128)} %weight_ref.3, ...), custom_call_target="tpu_custom_call" | custom-call | flops 8589934592 | bytes 1048576 | tf_op jit(solution)/shard_map/pallas_call | solution.py:570
  69.5 4.1 %all-to-all-done.1.refs_0_ = bf16[128,16,128]{2,1,0:T(8,128)(2,1)S(1)} async-done(((bf16[128,16,128]{2,1,0:T(8,128)(2,1)}), bf16[128,16,128]{2,1,0:T(8,128)(2,1)S(1)}, u32[]{:S(2)}, u32[]{:S(2)}) %all-to-all-start.1) | async-done | bytes 524320 | tf_op jit(solution)/shard_map/all_to_all | solution.py:576
  73.6 0.9 copy-done
  74.5 0.2 shard_map.134
  74.7 22.3 %all_to_all.15.arrived_ref = bf16[128,24,128]{2,1,0:T(8,128)(2,1)S(1)} all-to-all(bf16[128,24,128]{2,1,0:T(8,128)(2,1)S(1)} %shard_map.134), channel_id=1, replica_groups=mesh['gx'=16,'gy'=8] {'gx','gy'}, dimensions={0} | all-to-all | bytes 1572864 | tf_op jit(solution)/shard_map/all_to_all | solution.py:576
  97.1 1.7 %shard_map.135 = (f32[4096,64]{1,0:T(8,128)}, f32[16,64]{1,0:T(8,128)}) custom-call(bf16[128,24,128]{2,1,0:T(8,128)(2,1)S(1)} %all_to_all.15.arrived_ref), custom_call_target="tpu_custom_call" | custom-call | flops 268435456 | bytes 1048576 | tf_op jit(solution)/shard_map/pallas_call | solution.py:607
  (5 shorter events, 0.0 us)
Async XLA Ops:
  5.1 11.5 %copy-start.3 = (f32[64]{0:T(128)S(1)}, f32[64]{0:T(128)}, u32[]{:S(2)}) copy-start(f32[64]{0:T(128)} %param.13) | copy-start | bytes 772
  5.1 12.2 %copy-start.4 = (f32[64]{0:T(128)S(1)}, f32[64]{0:T(128)}, u32[]{:S(2)}) copy-start(f32[64]{0:T(128)} %param.15) | copy-start | bytes 772
  5.1 12.8 %copy-start.2 = (bf16[3,3,3,8,64]{4,3,2,1,0:T(8,128)(2,1)S(1)}, bf16[3,3,3,8,64]{4,3,2,1,0:T(8,128)(2,1)}, u32[]{:S(2)}) copy-start(bf16[3,3,3,8,64]{4,3,2,1,0:T(8,128)(2,1)} %param.12) | copy-start | bytes 82948
  5.1 33.8 %all-to-all-start = ((bf16[128,40,128]{2,1,0:T(8,128)(2,1)}), bf16[128,40,128]{2,1,0:T(8,128)(2,1)S(1)}, u32[]{:S(2)}, u32[]{:S(2)}) async-start(bf16[128,40,128]{2,1,0:T(8,128)(2,1)} %bitcast.10), calls=%async_computation | async-start | bytes 2621440 | tf_op jit(solution)/shard_map/all_to_all | solution.py:576
  38.9 1.1 %copy-start.1 = (bf16[128,40,128]{2,1,0:T(8,128)(2,1)}, bf16[128,40,128]{2,1,0:T(8,128)(2,1)S(1)}, u32[]{:S(2)}) copy-start(bf16[128,40,128]{2,1,0:T(8,128)(2,1)S(1)} %all-to-all-done.arrived_ref) | copy-start | bytes 3932164
  55.7 17.9 %all-to-all-start.1 = ((bf16[128,16,128]{2,1,0:T(8,128)(2,1)}), bf16[128,16,128]{2,1,0:T(8,128)(2,1)S(1)}, u32[]{:S(2)}, u32[]{:S(2)}) async-start(bf16[128,16,128]{2,1,0:T(8,128)(2,1)} %get-tuple-element.29), calls=%async_computation.1 | async-start | bytes 1048576 | tf_op jit(solution)/shard_map/all_to_all | solution.py:576
  73.6 1.0 copy-start

commit v4 on v3

--- a/solution.py
+++ b/solution.py
@@ -46,18 +46,14 @@
     y = 16 * b - 2 + t
     target = jnp.where((y >= 0) & (y < 128), group * 128 + y, -1)
     windows = ones_where(iota((320, 256), 1) == target)
-    empty = jnp.zeros((128, 128), BF)
-
-    def plane(j):
-        return jnp.concatenate([fields_ref[j], fields_ref[10 + j] if j < 6 else empty], axis=1)
-
-    lined = jnp.concatenate(
-        [
-            dot_nt(windows, jnp.concatenate([plane(2 * j), plane(2 * j + 1)], axis=0)).astype(BF)
-            for j in range(5)
-        ],
-        axis=1,
-    )
+    empty = jnp.zeros((64, 128), BF)
+
+    def plane(j, x):
+        return jnp.concatenate(
+            [fields_ref[j, x : x + 64, :], fields_ref[10 + j, x : x + 64, :] if j < 6 else empty],
+            axis=1,
+        )
+
     channel, lane = iota((64, 128), 0), iota((64, 128), 1)
     wells = wells_ref[...]
     placed = jnp.concatenate(
@@ -71,12 +67,29 @@
     extra = dot_nn(ones_where(iota((320, 32), 1) == target), placed)
     extra = jnp.concatenate([extra] * 4, axis=1)
     for part in range(4):
+        origin = min(max(32 * part - 16, 0), 64)
+        lined = jnp.concatenate(
+            [
+                dot_nt(
+                    windows, jnp.concatenate([plane(4 * n + j, origin) for j in range(4)], axis=0)
+                ).astype(BF)
+                for n in range(2)
+            ]
+            + [
+                dot_nt(
+                    windows, jnp.concatenate([plane(8 + j, origin) for j in range(2)], axis=0)
+                ).astype(BF)
+            ],
+            axis=1,
+        )
         lane = iota((1, 512), 1)
         within = lane & 127
         which = (within * 171) >> 11
         x = (lane >> 7) * 8 + 32 * part - 2 + within - 12 * which
-        target = jnp.where((which < 10) & (x >= 0) & (x < 128), which * 128 + x, -1)
-        spread = ones_where(iota((1280, 512), 0) == target)
+        target = jnp.where(
+            (which < 10) & (x >= 0) & (x < 128), which * 64 + x - origin, -1
+        )
+        spread = ones_where(iota((640, 512), 0) == target)
         blocks = (dot_nn(lined, spread) + extra).astype(BF)
         for a in range(4):
             out_ref[4 * part + a] = blocks[:, 128 * a : 128 * a + 128].reshape(8, 40, 128)
@@ -279,59 +292,34 @@
 
     lane = iota((16, 512), 1)
     start = jnp.where((iota((16, 512), 0) == 0) & (((lane >> 6) & 1) == 0), 0.0, 1.0)
-
-    def multiply(n, out_ref):
-        u = n // 3
-        v = 3 * (n - 3 * u)
-        near = pl.ds(pl.multiple_of(128 * v, 128), 384)
-        far = pl.ds(pl.multiple_of(128 * v + 128, 128), 384)
+    lane = iota((1, 512), 1)
+    px, py = lane >> 8, (lane >> 7) & 1
+    sides = {
+        ("u", 0): jnp.where((a == 0) & (px == 0), 0.0, 1.0),
+        ("u", 4): jnp.where((a == 15) & (px == 1), 0.0, 1.0),
+        ("v", 0): jnp.where((b == 0) & (py == 0), 0.0, 1.0),
+        ("v", 8): jnp.where((b == 7) & (py == 1), 0.0, 1.0),
+    }
+
+    def inside(value, u, v):
+        for key in (("u", u), ("v", v)):
+            if key in sides:
+                value = value * sides[key]
+        return value
+
+    def multiply(u, t, out_ref):
+        near, far = slice(384 * t, 384 * t + 384), slice(384 * t + 128, 384 * t + 512)
         both = jnp.concatenate(
             [shallow_ref[u, near], shallow_ref[u, far], deep_ref[u, near], deep_ref[u, far]], axis=1
         )
         out_ref[...] = dot_nn(both, big_ref[...])
 
-    def activate(n, in_ref):
-        u = n // 3
-        v = 3 * (n - 3 * u)
-        for t in range(3):
-            value = active(in_ref[128 * t : 128 * t + 128, :])
-            pairs_ref[u, v + t] = value.astype(BF)
-            pairs_ref[u, v + t, 0:16, :] = (value[0:16] * start).astype(BF)
-
-    multiply(0, even_ref)
-
-    def strips(n, carry):
-        multiply(2 * n + 1, odd_ref)
-        activate(2 * n, even_ref)
-        multiply(2 * n + 2, even_ref)
-        activate(2 * n + 1, odd_ref)
-        return carry
-
-    lax.fori_loop(0, 7, strips, 0)
-    activate(14, even_ref)
-
-    def clear(where, u, v, low):
-        @pl.when(where)
-        def _():
-            for lane in low:
-                shape = (5 if u is None else 1, 9 if v is None else 1, 128, 128)
-                pairs_ref[
-                    slice(None) if u is None else slice(u, u + 1),
-                    slice(None) if v is None else slice(v, v + 1),
-                    :,
-                    lane : lane + 128,
-                ] = jnp.zeros(shape, BF)
-
-    clear(a == 0, 0, None, (0, 128))
-    clear(a == 15, 4, None, (256, 384))
-    clear(b == 0, None, 0, (0, 256))
-    clear(b == 7, None, 8, (128, 384))
-
-    stores = [
-        pltpu.make_async_copy(pairs_ref.at[u], pairs_far.at[u], leave.at[u]) for u in range(5)
-    ]
-    for copy in stores:
-        copy.start()
+    def activate(u, t, in_ref):
+        for v in range(3 * t, 3 * t + 3):
+            at = 128 * (v - 3 * t)
+            value = inside(active(in_ref[at : at + 128, :]), u, v)
+            pairs_ref[u, v, 0:16, :] = (value[0:16] * start).astype(BF)
+            pairs_ref[u, v, 16:128, :] = value[16:128].astype(BF)
 
     row, lane = iota((80, 512), 0), iota((80, 512), 1)
     px, py, pz = lane >> 8, (lane >> 7) & 1, (lane >> 6) & 1
@@ -355,19 +343,35 @@
         edge = pltpu.roll(ends, shift, 1) if shift else ends
         edges += [none[0:64], edge.astype(BF)]
     sum_ref[...] = dot_nn(jnp.concatenate(edges, axis=0), last)
-    for u in range(5):
-        sides = [i for i in range(2) if 0 <= u - i < 4]
+
+    def gather(u):
+        layers = [i for i in range(2) if 0 <= u - i < 4]
         rows = []
-        for i in sides:
+        for i in layers:
             cot = cot_ref[:, 1024 * (u - i) : 1024 * (u - i) + 1024]
             rows += [
                 jnp.concatenate([cot, none], axis=1),
                 jnp.concatenate([none, cot], axis=1),
             ]
-        at = 256 * sides[0]
+        at = 256 * layers[0]
         sum_ref[at : at + 128 * len(rows), :] += dot_nn(
             jnp.concatenate(rows, axis=0), pairs_ref[u].reshape(1152, 512)
         )
+
+    slots = (even_ref, odd_ref)
+    stores = [
+        pltpu.make_async_copy(pairs_ref.at[u], pairs_far.at[u], leave.at[u]) for u in range(5)
+    ]
+    for n in range(16):
+        if n < 15:
+            multiply(n // 3, n % 3, slots[n % 2])
+        if n > 0:
+            activate((n - 1) // 3, (n - 1) % 3, slots[(n - 1) % 2])
+        if n > 3 and n % 3 == 1:
+            gather(n // 3 - 1)
+    for copy in stores:
+        copy.start()
+    gather(4)
     for r in range(32):
         for j in range(4):
             send_ref[4 * r + j] = sum_ref[16 * r : 16 * r + 16, 128 * j : 128 * j + 128].astype(BF)

time: 99.2 us -> 98.8 us (level)
  no operation moved by 1% of the time
where the time goes in v4:
time: 98.8 us; the launch traced here: 98.4 us
  Pallas kernels  38.5 us (39%)
  blocking collectives  22.3 us (23%)
  waiting for transfers between devices  16.7 us (17%)
  starting transfers between devices  15.4 us (16%)
  local copies, waits for them, and re-layouts  3.31 us (3%)
  other arithmetic  1.33 us (1%)
    all_to_all x1, blocking collectives, exchange(): return lax.all_to_all(blocks, AXES, split_axis=0, concat_axis=0, tiled=True)  22.3 us
    all_to_all x2, waiting for transfers between devices, exchange(): return lax.all_to_all(blocks, AXES, split_axis=0, concat_axis=0, tiled=True)  16.7 us
    pallas_call x1, Pallas kernels, lift(): call(lift_kernel, outs, scratch, spaces, (5, 5), cost=1 << 33, room=ROOM_...  15.6 us
    all_to_all x2, starting transfers between devices, exchange(): return lax.all_to_all(blocks, AXES, split_axis=0, concat_axis=0, tiled=True)  15.4 us
    pallas_call x1, Pallas kernels, coarsen(): call(coarse_kernel, outs, scratch, spaces, (7,), cost=1 << 33)  9.97 us
    pallas_call x1, Pallas kernels, prepare(): call(prep_kernel, outs, cost=1 << 32)  7.05 us
    pallas_call x1, Pallas kernels, pack(): call(pack_kernel, [((16, 8, 40, 128), BF)], cost=1 << 31)  4.01 us
    unnamed x10, local copies, waits for them, and re-layouts  2.07 us
  transfers between devices with their start and end apart: 2, of which 2 were waited for; matrix products, arithmetic and copies ran while one was open for 3% of the time, Pallas kernels for 17%

profile of v4, /device:TPU:1, one launch (start us, length us, event | category | flops | bytes accessed | tf_op | source)
XLA Modules:
  0.0 98.4 jit_solution(17613718294564227051)
XLA Ops:
  0.6 4.0 %shard_map.131 = bf16[16,8,40,128]{3,2,1,0:T(8,128)(2,1)} custom-call(bf16[16,128,128]{2,1,0:T(8,128)(2,1)} %bitcast.13, bf16[16,64]{1,0:T(8,128)(2,1)} %wells_ref.1), custom_call_target="tpu_custom_call" | custom-call | flops 2147483648 | bytes 1048576 | tf_op jit(solution)/shard_map/pallas_call | solution.py:504
  4.6 0.0 copy-start.3
  4.6 0.0 copy-start.4
  4.6 0.0 copy-start.2
  4.6 11.5 %all-to-all-start = ((bf16[128,40,128]{2,1,0:T(8,128)(2,1)}), bf16[128,40,128]{2,1,0:T(8,128)(2,1)S(1)}, u32[]{:S(2)}, u32[]{:S(2)}) async-start(bf16[128,40,128]{2,1,0:T(8,128)(2,1)} %bitcast.10), calls=%async_computation | async-start | bytes 2621440 | tf_op jit(solution)/shard_map/all_to_all | solution.py:580
  16.1 0.0 copy-done.3
  16.2 0.7 broadcast_in_dim_tile.6.bias_ref
  16.8 0.0 copy-done.4
  16.8 0.6 broadcast_in_dim_tile.7.bias_ref
  17.4 0.0 copy-done.2
  17.4 0.6 pad_add_fusion.tile_ref
  18.0 0.7 fusion.2.lift_ref
  18.8 7.0 %shard_map.130 = (bf16[4096,256]{1,0:T(8,128)(2,1)}, bf16[256,1024]{1,0:T(8,128)(2,1)}, f32[256,512]{1,0:T(8,128)}, bf16[1024,512]{1,0:T(8,128)(2,1)}, bf16[512,...) custom-call(s32[1,256]{1,0:T(1,128)} %well_ref.1, ...), custom_call_target="tpu_custom_call" | custom-call | flops 4294967296 | bytes 1048576 | tf_op jit(solution)/shard_map/pallas_call | solution.py:525
  25.8 12.7 %all-to-all-done.arrived_ref = bf16[128,40,128]{2,1,0:T(8,128)(2,1)S(1)} async-done(((bf16[128,40,128]{2,1,0:T(8,128)(2,1)}), bf16[128,40,128]{2,1,0:T(8,128)(2,1)S(1)}, u32[]{:S(2)}, u32[]{:S(2)}) %all-to-all-start) | async-done | bytes 1310752 | tf_op jit(solution)/shard_map/all_to_all | solution.py:580
  38.5 0.0 copy-start.1
  38.5 1.1 %copy-done.1 = bf16[128,40,128]{2,1,0:T(8,128)(2,1)} copy-done((bf16[128,40,128]{2,1,0:T(8,128)(2,1)}, bf16[128,40,128]{2,1,0:T(8,128)(2,1)S(1)}, u32[]{:S(2)}) %copy-start.1) | copy-done | bytes 1310744
  39.6 15.6 %shard_map.132 = (bf16[128,16,128]{2,1,0:T(8,128)(2,1)}, bf16[128,512]{1,0:T(8,128)(2,1)}, bf16[5,9,128,512]{3,2,1,0:T(8,128)(2,1)}) custom-call(s32[2]{0:T(128)} %pad_add_fusion.tile_ref, bf16[128,40,128]{2,1,0:T(8,128)(2,1)} %copy-done.1, f32[1,256]{1,0:T(1,128)} %weight_ref.3, f32[1,512]{1,0:T(1,128)} %broadcast_in_dim_tile.6.bias_ref, ...), custom_call_target="tpu_custom_call" | custom-call | flops 8589934592 | bytes 1048576 | tf_op jit(solution)/shard_map/pallas_call | solution.py:555
  55.2 3.9 %all-to-all-start.1 = ((bf16[128,16,128]{2,1,0:T(8,128)(2,1)}), bf16[128,16,128]{2,1,0:T(8,128)(2,1)S(1)}, u32[]{:S(2)}, u32[]{:S(2)}) async-start(bf16[128,16,128]{2,1,0:T(8,128)(2,1)} %get-tuple-element.29), calls=%async_computation.1 | async-start | bytes 1048576 | tf_op jit(solution)/shard_map/all_to_all | solution.py:580
  59.1 10.0 %shard_map.133 = (bf16[64,32,128]{2,1,0:T(8,128)(2,1)}, bf16[128,8,128]{2,1,0:T(8,128)(2,1)}) custom-call(bf16[512,512]{1,0:T(8,128)(2,1)} %get-tuple-element.18.taps_ref, bf16[128,512]{1,0:T(8,128)(2,1)} %get-tuple-element.25.last_ref, f32[1,128]{1,0:T(1,128)} %broadcast_in_dim_tile.7.bias_ref, f32[1,256]{1,0:T(1,128)} %weight_ref.3, ...), custom_call_target="tpu_custom_call" | custom-call | flops 8589934592 | bytes 1048576 | tf_op jit(solution)/shard_map/pallas_call | solution.py:574
  69.1 4.1 %all-to-all-done.1.refs_0_ = bf16[128,16,128]{2,1,0:T(8,128)(2,1)S(1)} async-done(((bf16[128,16,128]{2,1,0:T(8,128)(2,1)}), bf16[128,16,128]{2,1,0:T(8,128)(2,1)S(1)}, u32[]{:S(2)}, u32[]{:S(2)}) %all-to-all-start.1) | async-done | bytes 524320 | tf_op jit(solution)/shard_map/all_to_all | solution.py:580
  73.1 0.9 copy-done
  74.1 0.2 shard_map.134
  74.3 22.3 %all_to_all.15.arrived_ref = bf16[128,24,128]{2,1,0:T(8,128)(2,1)S(1)} all-to-all(bf16[128,24,128]{2,1,0:T(8,128)(2,1)S(1)} %shard_map.134), channel_id=1, replica_groups=mesh['gx'=16,'gy'=8] {'gx','gy'}, dimensions={0} | all-to-all | bytes 1572864 | tf_op jit(solution)/shard_map/all_to_all | solution.py:580
  96.6 1.7 %shard_map.135 = (f32[4096,64]{1,0:T(8,128)}, f32[16,64]{1,0:T(8,128)}) custom-call(bf16[128,24,128]{2,1,0:T(8,128)(2,1)S(1)} %all_to_all.15.arrived_ref), custom_call_target="tpu_custom_call" | custom-call | flops 268435456 | bytes 1048576 | tf_op jit(solution)/shard_map/pallas_call | solution.py:611
  (5 shorter events, 0.0 us)
Async XLA Ops:
  4.6 11.5 %copy-start.3 = (f32[64]{0:T(128)S(1)}, f32[64]{0:T(128)}, u32[]{:S(2)}) copy-start(f32[64]{0:T(128)} %param.13) | copy-start | bytes 772
  4.6 12.2 %copy-start.4 = (f32[64]{0:T(128)S(1)}, f32[64]{0:T(128)}, u32[]{:S(2)}) copy-start(f32[64]{0:T(128)} %param.15) | copy-start | bytes 772
  4.6 12.8 %copy-start.2 = (bf16[3,3,3,8,64]{4,3,2,1,0:T(8,128)(2,1)S(1)}, bf16[3,3,3,8,64]{4,3,2,1,0:T(8,128)(2,1)}, u32[]{:S(2)}) copy-start(bf16[3,3,3,8,64]{4,3,2,1,0:T(8,128)(2,1)} %param.12) | copy-start | bytes 82948
  4.6 33.8 %all-to-all-start = ((bf16[128,40,128]{2,1,0:T(8,128)(2,1)}), bf16[128,40,128]{2,1,0:T(8,128)(2,1)S(1)}, u32[]{:S(2)}, u32[]{:S(2)}) async-start(bf16[128,40,128]{2,1,0:T(8,128)(2,1)} %bitcast.10), calls=%async_computation | async-start | bytes 2621440 | tf_op jit(solution)/shard_map/all_to_all | solution.py:580
  38.5 1.1 %copy-start.1 = (bf16[128,40,128]{2,1,0:T(8,128)(2,1)}, bf16[128,40,128]{2,1,0:T(8,128)(2,1)S(1)}, u32[]{:S(2)}) copy-start(bf16[128,40,128]{2,1,0:T(8,128)(2,1)S(1)} %all-to-all-done.arrived_ref) | copy-start | bytes 3932164
  55.2 18.0 %all-to-all-start.1 = ((bf16[128,16,128]{2,1,0:T(8,128)(2,1)}), bf16[128,16,128]{2,1,0:T(8,128)(2,1)S(1)}, u32[]{:S(2)}, u32[]{:S(2)}) async-start(bf16[128,16,128]{2,1,0:T(8,128)(2,1)} %get-tuple-element.29), calls=%async_computation.1 | async-start | bytes 1048576 | tf_op jit(solution)/shard_map/all_to_all | solution.py:580
  73.1 1.0 copy-start

commit v5 on v4

--- a/solution.py
+++ b/solution.py
@@ -37,7 +37,7 @@
     return high, (x - high.astype(F32)).astype(BF)
 
 
-def pack_kernel(fields_ref, wells_ref, out_ref):
+def pack_kernel(fields_ref, wells_ref, far_ref, out_ref, leave):
     row = iota((320, 1), 0)
     b = (row * 205) >> 13
     rho = row - 40 * b
@@ -66,6 +66,12 @@
     target = jnp.where(t < 16, 16 * group + t, -1)
     extra = dot_nn(ones_where(iota((320, 32), 1) == target), placed)
     extra = jnp.concatenate([extra] * 4, axis=1)
+    stores = [
+        pltpu.make_async_copy(
+            out_ref.at[4 * n : 4 * n + 4], far_ref.at[4 * n : 4 * n + 4], leave.at[n]
+        )
+        for n in range(4)
+    ]
     for part in range(4):
         origin = min(max(32 * part - 16, 0), 64)
         lined = jnp.concatenate(
@@ -93,6 +99,9 @@
         blocks = (dot_nn(lined, spread) + extra).astype(BF)
         for a in range(4):
             out_ref[4 * part + a] = blocks[:, 128 * a : 128 * a + 128].reshape(8, 40, 128)
+        stores[part].start()
+    for copy in stores:
+        copy.wait()
 
 
 def prep_kernel(
@@ -182,10 +191,10 @@
 
 def lift_kernel(
     tile_ref,
-    arrived_ref,
     weight_ref,
     bias_ref,
-    lanes_ref,
+    arrived_far,
+    lanes_far,
     cells_far,
     rows_far,
     half_far,
@@ -208,6 +217,8 @@
     half_ref,
     big_ref,
     grad_ref,
+    arrived_ref,
+    lanes_ref,
     arrive,
     leave,
 ):
@@ -216,6 +227,9 @@
         pltpu.make_async_copy(source, target, arrive.at[n])
         for n, (source, target) in enumerate(
             [
+                (arrived_far.at[0:64], arrived_ref.at[0:64]),
+                (arrived_far.at[64:128], arrived_ref.at[64:128]),
+                (lanes_far, lanes_ref),
                 (rows_far, rows_ref),
                 (half_far, half_ref),
                 (cells_far, cells_ref),
@@ -229,8 +243,9 @@
 
     row, col = iota((256, 256), 0), iota((256, 256), 1)
     turn = ones_where(col == (row & 31) * 8 + (row >> 5))
-    for tile in range(5):
-        for pair in range(2):
+    for pair in range(2):
+        fetch[pair].wait()
+        for tile in range(5):
             block = jnp.concatenate(
                 [
                     arrived_ref[32 * s : 32 * s + 32, 8 * tile : 8 * tile + 8].reshape(256, 128)
@@ -248,6 +263,7 @@
                         32 * r : 32 * r + 32, 128 * s : 128 * s + 128
                     ]
 
+    fetch[2].wait()
     end_ref[...] = jnp.zeros((5, 16, 256), F32)
     first = iota((128, 640), 0) == 0
     for half in range(2):
@@ -266,7 +282,7 @@
                 if y2 > 0:
                     end_ref[u, y2 - 1 : y2, 128:256] = part[127:128, lane : lane + 128]
 
-    for copy in fetch:
+    for copy in fetch[3:]:
         copy.wait()
     lane, channel = iota((64, 512), 1) & 255, iota((64, 512), 0)
     fold = ones_where(lane == jnp.where(channel < 56, channel + 200, channel + 64))
@@ -367,10 +383,10 @@
             multiply(n // 3, n % 3, slots[n % 2])
         if n > 0:
             activate((n - 1) // 3, (n - 1) % 3, slots[(n - 1) % 2])
+        if n > 0 and n % 3 == 0:
+            stores[n // 3 - 1].start()
         if n > 3 and n % 3 == 1:
             gather(n // 3 - 1)
-    for copy in stores:
-        copy.start()
     gather(4)
     for r in range(32):
         for j in range(4):
@@ -464,20 +480,24 @@
 
 
 def finish_kernel(arrived_ref, grad_ref, feat_ref):
+    tap = pl.program_id(0)
+    a, px = tap // 2, tap % 2
     eye = ones_where(iota((128, 128), 0) == iota((128, 128), 1))
-    for a in range(2):
-        for b in range(2):
+    for b in range(2):
+        for py in range(2):
             for d in range(2):
-                base = 4 * (4 * a + 2 * b + d)
-                for p in range(4):
-                    block = jnp.concatenate(
-                        [arrived_ref[4 * (base + t) + p, 0:16, :] for t in range(4)], axis=0
-                    )
-                    tap = ((2 * a + p // 2) * 4 + 2 * b + p % 2) * 4 + 2 * d
-                    grad_ref[64 * tap : 64 * tap + 128, :] = dot_nt(eye, block)
-    feat = jnp.sum(arrived_ref[:, 16:24, :].astype(F32), axis=0)
-    feat_ref[0:8, :] = feat[:, 0:64]
-    feat_ref[8:16, :] = pltpu.roll(feat, 64, 1)[:, 0:64]
+                base = 16 * (4 * a + 2 * b + d) + 2 * px + py
+                block = jnp.concatenate(
+                    [arrived_ref[base + 4 * t, 0:16, :] for t in range(4)], axis=0
+                )
+                at = 256 * (2 * b + py) + 128 * d
+                grad_ref[at : at + 128, :] = dot_nt(eye, block)
+
+    @pl.when(tap == 0)
+    def _():
+        feat = jnp.sum(arrived_ref[:, 16:24, :].astype(F32), axis=0)
+        feat_ref[0:8, :] = feat[:, 0:64]
+        feat_ref[8:16, :] = pltpu.roll(feat, 64, 1)[:, 0:64]
 
 
 VMEM, SMEM, HBM = pltpu.VMEM, pltpu.SMEM, pltpu.HBM
@@ -501,7 +521,8 @@
 
 
 def pack(fields, well_grad):
-    return call(pack_kernel, [((16, 8, 40, 128), BF)], cost=1 << 31)(
+    outs = [((16, 8, 40, 128), BF)]
+    return call(pack_kernel, outs, outs, [VMEM, VMEM, HBM], (4,), cost=1 << 31)(
         fields.reshape(16, 128, 128), well_grad
     )[0].reshape(128, 40, 128)
 
@@ -549,11 +570,13 @@
         ((256, 512), F32),
         ((512, 512), BF),
         ((64, 4096), F32),
-    ]
-    spaces = [SMEM] + [VMEM] * 4 + [HBM] * 5 + [VMEM, VMEM, HBM]
+        ((128, 40, 128), BF),
+        ((512, 640), BF),
+    ]
+    spaces = [SMEM] + [VMEM] * 2 + [HBM] * 7 + [VMEM, VMEM, HBM]
     bias = jnp.tile(0.5 * b_lift, 8)[None, :]
-    return call(lift_kernel, outs, scratch, spaces, (5, 5), cost=1 << 33, room=ROOM_LIFT)(
-        tile, arrived, perf_weight, bias, lanes, cells, rows, half, big, grad
+    return call(lift_kernel, outs, scratch, spaces, (8, 5), cost=1 << 33, room=ROOM_LIFT)(
+        tile, perf_weight, bias, arrived, lanes, cells, rows, half, big, grad
     )
 
 
@@ -574,6 +597,24 @@
     return call(coarse_kernel, outs, scratch, spaces, (7,), cost=1 << 33)(
         taps, last, bias, perf_weight, pairs, cells, owner
     )
+
+
+def finish(shared):
+    return pl.pallas_call(
+        finish_kernel,
+        out_shape=[
+            jax.ShapeDtypeStruct((4096, 64), F32),
+            jax.ShapeDtypeStruct((16, 64), F32),
+        ],
+        grid=(4,),
+        in_specs=[pl.BlockSpec((128, 24, 128), lambda i: (0, 0, 0))],
+        out_specs=[
+            pl.BlockSpec((1024, 64), lambda i: (i, 0)),
+            pl.BlockSpec((16, 64), lambda i: (0, 0)),
+        ],
+        compiler_params=pltpu.CompilerParams(vmem_limit_bytes=8 << 20),
+        interpret=INTERPRET,
+    )(shared)
 
 
 def exchange(blocks):
@@ -608,9 +649,7 @@
         lambda *refs: sum_kernel(scale, *refs), [((128, 24, 128), BF)], cost=1 << 20, room=8
     )(parts, feat)[0]
     shared = exchange(shared)
-    down_grad, well_feat = call(
-        finish_kernel, [((4096, 64), F32), ((16, 64), F32)], cost=1 << 28, room=8
-    )(shared)
+    down_grad, well_feat = finish(shared)
     return (
         coarse.reshape(64, 4, 8, 128),
         well_feat,

time: 98.8 us -> 97.7 us (0.989)
  Pallas kernels: 38.5 us -> 37.4 us
    pallas_call x3, Pallas kernels: 21.3 us -> 20.2 us  [the longest x1 14 us: lift(): call(lift_kernel, outs, scratch, spaces, (8, 5), cost=1 << 33, room=ROOM_...]
where the time goes in v5:
time: 97.7 us; the launch traced here: 97.3 us
  Pallas kernels  37.4 us (38%)
  blocking collectives  22.3 us (23%)
  waiting for transfers between devices  16.6 us (17%)
  starting transfers between devices  15.6 us (16%)
  local copies, waits for them, and re-layouts  3.32 us (3%)
  other arithmetic  1.33 us (1%)
    all_to_all x1, blocking collectives, exchange(): return lax.all_to_all(blocks, AXES, split_axis=0, concat_axis=0, tiled=True)  22.3 us
    all_to_all x2, waiting for transfers between devices, exchange(): return lax.all_to_all(blocks, AXES, split_axis=0, concat_axis=0, tiled=True)  16.6 us
    all_to_all x2, starting transfers between devices, exchange(): return lax.all_to_all(blocks, AXES, split_axis=0, concat_axis=0, tiled=True)  15.6 us
    pallas_call x1, Pallas kernels, lift(): call(lift_kernel, outs, scratch, spaces, (8, 5), cost=1 << 33, room=ROOM_...  14 us
    pallas_call x1, Pallas kernels, coarsen(): call(coarse_kernel, outs, scratch, spaces, (7,), cost=1 << 33)  9.97 us
    pallas_call x1, Pallas kernels, prepare(): call(prep_kernel, outs, cost=1 << 32)  7.05 us
    pallas_call x1, Pallas kernels, pack(): call(pack_kernel, outs, outs, [VMEM, VMEM, HBM], (4,), cost=1 << 31)  3.71 us
    pallas_call x1, Pallas kernels, finish(): pl.pallas_call(finish_kernel, out_shape=[jax.ShapeDtypeStruct((4096, 64),...  2.44 us
  transfers between devices with their start and end apart: 2, of which 2 were waited for; matrix products, arithmetic and copies ran while one was open for 3% of the time, Pallas kernels for 17%

profile of v5, /device:TPU:1, one launch (start us, length us, event | category | flops | bytes accessed | tf_op | source)
XLA Modules:
  0.0 97.3 jit_solution(10389817155642730409)
XLA Ops:
  0.6 3.7 %shard_map.131 = bf16[16,8,40,128]{3,2,1,0:T(8,128)(2,1)} custom-call(bf16[16,128,128]{2,1,0:T(8,128)(2,1)} %bitcast.14, bf16[16,64]{1,0:T(8,128)(2,1)} %wells_ref.1), custom_call_target="tpu_custom_call" | custom-call | flops 2147483648 | bytes 1048576 | tf_op jit(solution)/shard_map/pallas_call | solution.py:525
  4.3 0.0 copy-start.3
  4.4 0.0 copy-start.4
  4.4 0.0 copy-start.2
  4.4 11.7 %all-to-all-start = ((bf16[128,40,128]{2,1,0:T(8,128)(2,1)}), bf16[128,40,128]{2,1,0:T(8,128)(2,1)S(1)}, u32[]{:S(2)}, u32[]{:S(2)}) async-start(bf16[128,40,128]{2,1,0:T(8,128)(2,1)} %bitcast.10), calls=%async_computation | async-start | bytes 2621440 | tf_op jit(solution)/shard_map/all_to_all | solution.py:621
  16.1 0.0 copy-done.3
  16.1 0.7 broadcast_in_dim_tile.6.bias_ref
  16.8 0.0 copy-done.4
  16.8 0.6 broadcast_in_dim_tile.7.bias_ref
  17.3 0.0 copy-done.2
  17.3 0.6 pad_add_fusion.tile_ref
  17.9 0.7 fusion.2.lift_ref
  18.7 7.0 %shard_map.130 = (bf16[4096,256]{1,0:T(8,128)(2,1)}, bf16[256,1024]{1,0:T(8,128)(2,1)}, f32[256,512]{1,0:T(8,128)}, bf16[1024,512]{1,0:T(8,128)(2,1)}, bf16[512,...) custom-call(s32[1,256]{1,0:T(1,128)} %well_ref.1, ...), custom_call_target="tpu_custom_call" | custom-call | flops 4294967296 | bytes 1048576 | tf_op jit(solution)/shard_map/pallas_call | solution.py:546
  25.7 12.5 %all-to-all-done.arrived_far = bf16[128,40,128]{2,1,0:T(8,128)(2,1)S(1)} async-done(((bf16[128,40,128]{2,1,0:T(8,128)(2,1)}), bf16[128,40,128]{2,1,0:T(8,128)(2,1)S(1)}, u32[]{:S(2)}, u32[]{:S(2)}) %all-to-all-start) | async-done | bytes 1310752 | tf_op jit(solution)/shard_map/all_to_all | solution.py:621
  38.2 0.0 copy-start.1
  38.2 1.1 %copy-done.1 = bf16[128,40,128]{2,1,0:T(8,128)(2,1)} copy-done((bf16[128,40,128]{2,1,0:T(8,128)(2,1)}, bf16[128,40,128]{2,1,0:T(8,128)(2,1)S(1)}, u32[]{:S(2)}) %copy-start.1) | copy-done | bytes 1310744
  39.3 14.0 %shard_map.132 = (bf16[128,16,128]{2,1,0:T(8,128)(2,1)}, bf16[128,512]{1,0:T(8,128)(2,1)}, bf16[5,9,128,512]{3,2,1,0:T(8,128)(2,1)}) custom-call(s32[2]{0:T(128)} %pad_add_fusion.tile_ref, f32[1,256]{1,0:T(1,128)} %weight_ref.3, f32[1,512]{1,0:T(1,128)} %broadcast_in_dim_tile.6.bias_ref, bf16[128,40,128]{2,1,0:T(8,128)(2,1)} %copy-done.1, ...), custom_call_target="tpu_custom_call" | custom-call | flops 8589934592 | bytes 1048576 | tf_op jit(solution)/shard_map/pallas_call | solution.py:578
  53.4 3.9 %all-to-all-start.1 = ((bf16[128,16,128]{2,1,0:T(8,128)(2,1)}), bf16[128,16,128]{2,1,0:T(8,128)(2,1)S(1)}, u32[]{:S(2)}, u32[]{:S(2)}) async-start(bf16[128,16,128]{2,1,0:T(8,128)(2,1)} %get-tuple-element.29), calls=%async_computation.1 | async-start | bytes 1048576 | tf_op jit(solution)/shard_map/all_to_all | solution.py:621
  57.3 10.0 %shard_map.133 = (bf16[64,32,128]{2,1,0:T(8,128)(2,1)}, bf16[128,8,128]{2,1,0:T(8,128)(2,1)}) custom-call(bf16[512,512]{1,0:T(8,128)(2,1)} %get-tuple-element.18.taps_ref, bf16[128,512]{1,0:T(8,128)(2,1)} %get-tuple-element.25.last_ref, f32[1,128]{1,0:T(1,128)} %broadcast_in_dim_tile.7.bias_ref, f32[1,256]{1,0:T(1,128)} %weight_ref.3, ...), custom_call_target="tpu_custom_call" | custom-call | flops 8589934592 | bytes 1048576 | tf_op jit(solution)/shard_map/pallas_call | solution.py:597
  67.3 4.1 %all-to-all-done.1.refs_0_ = bf16[128,16,128]{2,1,0:T(8,128)(2,1)S(1)} async-done(((bf16[128,16,128]{2,1,0:T(8,128)(2,1)}), bf16[128,16,128]{2,1,0:T(8,128)(2,1)S(1)}, u32[]{:S(2)}, u32[]{:S(2)}) %all-to-all-start.1) | async-done | bytes 524320 | tf_op jit(solution)/shard_map/all_to_all | solution.py:621
  71.3 0.9 copy-done
  72.3 0.2 shard_map.134
  72.5 22.3 %all_to_all.15.arrived_ref = bf16[128,24,128]{2,1,0:T(8,128)(2,1)S(1)} all-to-all(bf16[128,24,128]{2,1,0:T(8,128)(2,1)S(1)} %shard_map.134), channel_id=1, replica_groups=mesh['gx'=16,'gy'=8] {'gx','gy'}, dimensions={0} | all-to-all | bytes 1572864 | tf_op jit(solution)/shard_map/all_to_all | solution.py:621
  94.8 2.4 %shard_map.135 = (f32[4096,64]{1,0:T(8,128)}, f32[16,64]{1,0:T(8,128)}) custom-call(bf16[128,24,128]{2,1,0:T(8,128)(2,1)S(1)} %all_to_all.15.arrived_ref), custom_call_target="tpu_custom_call" | custom-call | tf_op jit(solution)/shard_map/pallas_call | solution.py:603
  (5 shorter events, 0.0 us)
Async XLA Ops:
  4.3 11.7 %copy-start.3 = (f32[64]{0:T(128)S(1)}, f32[64]{0:T(128)}, u32[]{:S(2)}) copy-start(f32[64]{0:T(128)} %param.13) | copy-start | bytes 772
  4.4 12.4 %copy-start.4 = (f32[64]{0:T(128)S(1)}, f32[64]{0:T(128)}, u32[]{:S(2)}) copy-start(f32[64]{0:T(128)} %param.15) | copy-start | bytes 772
  4.4 13.0 %copy-start.2 = (bf16[3,3,3,8,64]{4,3,2,1,0:T(8,128)(2,1)S(1)}, bf16[3,3,3,8,64]{4,3,2,1,0:T(8,128)(2,1)}, u32[]{:S(2)}) copy-start(bf16[3,3,3,8,64]{4,3,2,1,0:T(8,128)(2,1)} %param.12) | copy-start | bytes 82948
  4.4 33.8 %all-to-all-start = ((bf16[128,40,128]{2,1,0:T(8,128)(2,1)}), bf16[128,40,128]{2,1,0:T(8,128)(2,1)S(1)}, u32[]{:S(2)}, u32[]{:S(2)}) async-start(bf16[128,40,128]{2,1,0:T(8,128)(2,1)} %bitcast.10), calls=%async_computation | async-start | bytes 2621440 | tf_op jit(solution)/shard_map/all_to_all | solution.py:621
  38.2 1.1 %copy-start.1 = (bf16[128,40,128]{2,1,0:T(8,128)(2,1)}, bf16[128,40,128]{2,1,0:T(8,128)(2,1)S(1)}, u32[]{:S(2)}) copy-start(bf16[128,40,128]{2,1,0:T(8,128)(2,1)S(1)} %all-to-all-done.arrived_far) | copy-start | bytes 3932164
  53.4 18.0 %all-to-all-start.1 = ((bf16[128,16,128]{2,1,0:T(8,128)(2,1)}), bf16[128,16,128]{2,1,0:T(8,128)(2,1)S(1)}, u32[]{:S(2)}, u32[]{:S(2)}) async-start(bf16[128,16,128]{2,1,0:T(8,128)(2,1)} %get-tuple-element.29), calls=%async_computation.1 | async-start | bytes 1048576 | tf_op jit(solution)/shard_map/all_to_all | solution.py:621
  71.3 1.0 copy-start

commit v6 on v5

--- a/solution.py
+++ b/solution.py
@@ -137,7 +137,7 @@
     column = jnp.transpose(jnp.broadcast_to(slot, (128, 256)).astype(F32))[:, 0:1].astype(I32)
     place = jnp.where(column >= 0, ((column & 15) >> 1) * 128 + (column >> 4), -1)
     rows_ref[...] = ones_where(iota((256, 1024), 1) == place)
-    half_ref[...] = jnp.where((iota((256, 512), 1) >> 8) == (column & 1), 1.0, 0.0)
+    half_ref[...] = ones_where((iota((256, 512), 1) >> 8) == (column & 1))
 
     lane = iota((1, 640), 1)
     plane = lane & 15
@@ -186,7 +186,7 @@
         for uv in range(32):
             grad_ref[8 * g : 8 * g + 8, 128 * uv : 128 * uv + 128] = part[
                 8 * uv : 8 * uv + 8
-            ]
+            ].astype(BF)
 
 
 def lift_kernel(
@@ -286,10 +286,10 @@
         copy.wait()
     lane, channel = iota((64, 512), 1) & 255, iota((64, 512), 0)
     fold = ones_where(lane == jnp.where(channel < 56, channel + 200, channel + 64))
-    pulled = (dot_nn(rows_ref[...], sorted_ref[0:1024, :]) * half_ref[...]).astype(BF)
+    pulled = (dot_nn(rows_ref[...], sorted_ref[0:1024, :]) * half_ref[...].astype(F32)).astype(BF)
     spread = dot_nt(fold, pulled) * weight_ref[...]
     added = dot_nt(jnp.concatenate(split(spread), axis=0), cells_ref[...])
-    grown = (grad_ref[...] + added[0:64] + added[64:128]).astype(BF)
+    grown = (grad_ref[...].astype(F32) + added[0:64] + added[64:128]).astype(BF)
     cot_ref[0:64, :] = grown
     lane = iota((64, 128), 1)
     ends = jnp.zeros((64, 128), F32)
@@ -480,24 +480,20 @@
 
 
 def finish_kernel(arrived_ref, grad_ref, feat_ref):
-    tap = pl.program_id(0)
-    a, px = tap // 2, tap % 2
     eye = ones_where(iota((128, 128), 0) == iota((128, 128), 1))
-    for b in range(2):
-        for py in range(2):
+    for a in range(2):
+        for b in range(2):
             for d in range(2):
-                base = 16 * (4 * a + 2 * b + d) + 2 * px + py
-                block = jnp.concatenate(
-                    [arrived_ref[base + 4 * t, 0:16, :] for t in range(4)], axis=0
-                )
-                at = 256 * (2 * b + py) + 128 * d
-                grad_ref[at : at + 128, :] = dot_nt(eye, block)
-
-    @pl.when(tap == 0)
-    def _():
-        feat = jnp.sum(arrived_ref[:, 16:24, :].astype(F32), axis=0)
-        feat_ref[0:8, :] = feat[:, 0:64]
-        feat_ref[8:16, :] = pltpu.roll(feat, 64, 1)[:, 0:64]
+                base = 4 * (4 * a + 2 * b + d)
+                for p in range(4):
+                    block = jnp.concatenate(
+                        [arrived_ref[4 * (base + t) + p, 0:16, :] for t in range(4)], axis=0
+                    )
+                    tap = ((2 * a + p // 2) * 4 + 2 * b + p % 2) * 4 + 2 * d
+                    grad_ref[64 * tap : 64 * tap + 128, :] = dot_nt(eye, block)
+    feat = jnp.sum(arrived_ref[:, 16:24, :].astype(F32), axis=0)
+    feat_ref[0:8, :] = feat[:, 0:64]
+    feat_ref[8:16, :] = pltpu.roll(feat, 64, 1)[:, 0:64]
 
 
 VMEM, SMEM, HBM = pltpu.VMEM, pltpu.SMEM, pltpu.HBM
@@ -536,12 +532,12 @@
     outs = [
         ((4096, 256), BF),
         ((256, 1024), BF),
-        ((256, 512), F32),
+        ((256, 512), BF),
         ((1024, 512), BF),
         ((512, 640), BF),
         ((512, 512), BF),
         ((512, 512), BF),
-        ((64, 4096), F32),
+        ((64, 4096), BF),
     ]
     return call(prep_kernel, outs, cost=1 << 32)(
         perf_well,
@@ -567,9 +563,9 @@
         ((5, 9, 128, 512), BF),
         ((4096, 256), BF),
         ((256, 1024), BF),
-        ((256, 512), F32),
+        ((256, 512), BF),
         ((512, 512), BF),
-        ((64, 4096), F32),
+        ((64, 4096), BF),
         ((128, 40, 128), BF),
         ((512, 640), BF),
     ]
@@ -600,21 +596,8 @@
 
 
 def finish(shared):
-    return pl.pallas_call(
-        finish_kernel,
-        out_shape=[
-            jax.ShapeDtypeStruct((4096, 64), F32),
-            jax.ShapeDtypeStruct((16, 64), F32),
-        ],
-        grid=(4,),
-        in_specs=[pl.BlockSpec((128, 24, 128), lambda i: (0, 0, 0))],
-        out_specs=[
-            pl.BlockSpec((1024, 64), lambda i: (i, 0)),
-            pl.BlockSpec((16, 64), lambda i: (0, 0)),
-        ],
-        compiler_params=pltpu.CompilerParams(vmem_limit_bytes=8 << 20),
-        interpret=INTERPRET,
-    )(shared)
+    outs = [((4096, 64), F32), ((16, 64), F32)]
+    return call(finish_kernel, outs, cost=1 << 28, room=8)(shared)
 
 
 def exchange(blocks):

time: 97.7 us -> 97 us (level)
  Pallas kernels: 37.4 us -> 36.3 us
where the time goes in v6:
time: 97 us; the launch traced here: 96.6 us
  Pallas kernels  36.3 us (37%)
  blocking collectives  22.3 us (23%)
  waiting for transfers between devices  17 us (18%)
  starting transfers between devices  15.6 us (16%)
  local copies, waits for them, and re-layouts  3.32 us (3%)
  other arithmetic  1.31 us (1%)
    all_to_all x1, blocking collectives, exchange(): return lax.all_to_all(blocks, AXES, split_axis=0, concat_axis=0, tiled=True)  22.3 us
    all_to_all x2, waiting for transfers between devices, exchange(): return lax.all_to_all(blocks, AXES, split_axis=0, concat_axis=0, tiled=True)  17 us
    all_to_all x2, starting transfers between devices, exchange(): return lax.all_to_all(blocks, AXES, split_axis=0, concat_axis=0, tiled=True)  15.6 us
    pallas_call x1, Pallas kernels, lift(): call(lift_kernel, outs, scratch, spaces, (8, 5), cost=1 << 33, room=ROOM_...  14.1 us
    pallas_call x1, Pallas kernels, coarsen(): call(coarse_kernel, outs, scratch, spaces, (7,), cost=1 << 33)  9.97 us
    pallas_call x1, Pallas kernels, prepare(): call(prep_kernel, outs, cost=1 << 32)  6.67 us
    pallas_call x1, Pallas kernels, pack(): call(pack_kernel, outs, outs, [VMEM, VMEM, HBM], (4,), cost=1 << 31)  3.71 us
    unnamed x10, local copies, waits for them, and re-layouts  2.08 us
  transfers between devices with their start and end apart: 2, of which 2 were waited for; matrix products, arithmetic and copies ran while one was open for 3% of the time, Pallas kernels for 17%

profile of v6, /device:TPU:1, one launch (start us, length us, event | category | flops | bytes accessed | tf_op | source)
XLA Modules:
  0.0 96.6 jit_solution(5942717613235667034)
XLA Ops:
  0.6 3.7 %shard_map.131 = bf16[16,8,40,128]{3,2,1,0:T(8,128)(2,1)} custom-call(bf16[16,128,128]{2,1,0:T(8,128)(2,1)} %bitcast.13, bf16[16,64]{1,0:T(8,128)(2,1)} %wells_ref.1), custom_call_target="tpu_custom_call" | custom-call | flops 2147483648 | bytes 1048576 | tf_op jit(solution)/shard_map/pallas_call | solution.py:521
  4.3 0.0 copy-start.3
  4.4 0.0 copy-start.4
  4.4 0.0 copy-start.2
  4.4 11.7 %all-to-all-start = ((bf16[128,40,128]{2,1,0:T(8,128)(2,1)}), bf16[128,40,128]{2,1,0:T(8,128)(2,1)S(1)}, u32[]{:S(2)}, u32[]{:S(2)}) async-start(bf16[128,40,128]{2,1,0:T(8,128)(2,1)} %bitcast.10), calls=%async_computation | async-start | bytes 2621440 | tf_op jit(solution)/shard_map/all_to_all | solution.py:604
  16.1 0.0 copy-done.3
  16.1 0.7 broadcast_in_dim_tile.6.bias_ref
  16.8 0.0 copy-done.4
  16.8 0.6 broadcast_in_dim_tile.7.bias_ref
  17.3 0.0 copy-done.2
  17.3 0.6 pad_add_fusion.tile_ref
  17.9 0.7 fusion.2.lift_ref
  18.6 6.7 %shard_map.130 = (bf16[4096,256]{1,0:T(8,128)(2,1)}, bf16[256,1024]{1,0:T(8,128)(2,1)}, bf16[256,512]{1,0:T(8,128)(2,1)}, bf16[1024,512]{1,0:T(8,128)(2,1)}, bf1...) custom-call(s32[1,256]{1,0:T(1,128)} %well_ref.1, ...), custom_call_target="tpu_custom_call" | custom-call | flops 4294967296 | bytes 1048576 | tf_op jit(solution)/shard_map/pallas_call | solution.py:542
  25.3 12.9 %all-to-all-done.arrived_far = bf16[128,40,128]{2,1,0:T(8,128)(2,1)S(1)} async-done(((bf16[128,40,128]{2,1,0:T(8,128)(2,1)}), bf16[128,40,128]{2,1,0:T(8,128)(2,1)S(1)}, u32[]{:S(2)}, u32[]{:S(2)}) %all-to-all-start) | async-done | bytes 1310752 | tf_op jit(solution)/shard_map/all_to_all | solution.py:604
  38.2 0.0 copy-start.1
  38.2 1.1 %copy-done.1 = bf16[128,40,128]{2,1,0:T(8,128)(2,1)} copy-done((bf16[128,40,128]{2,1,0:T(8,128)(2,1)}, bf16[128,40,128]{2,1,0:T(8,128)(2,1)S(1)}, u32[]{:S(2)}) %copy-start.1) | copy-done | bytes 1310744
  39.3 14.1 %shard_map.132 = (bf16[128,16,128]{2,1,0:T(8,128)(2,1)}, bf16[128,512]{1,0:T(8,128)(2,1)}, bf16[5,9,128,512]{3,2,1,0:T(8,128)(2,1)}) custom-call(s32[2]{0:T(128)} %pad_add_fusion.tile_ref, f32[1,256]{1,0:T(1,128)} %weight_ref.3, f32[1,512]{1,0:T(1,128)} %broadcast_in_dim_tile.6.bias_ref, bf16[128,40,128]{2,1,0:T(8,128)(2,1)} %copy-done.1, ...), custom_call_target="tpu_custom_call" | custom-call | flops 8589934592 | bytes 1048576 | tf_op jit(solution)/shard_map/pallas_call | solution.py:574
  53.4 3.9 %all-to-all-start.1 = ((bf16[128,16,128]{2,1,0:T(8,128)(2,1)}), bf16[128,16,128]{2,1,0:T(8,128)(2,1)S(1)}, u32[]{:S(2)}, u32[]{:S(2)}) async-start(bf16[128,16,128]{2,1,0:T(8,128)(2,1)} %get-tuple-element.29), calls=%async_computation.1 | async-start | bytes 1048576 | tf_op jit(solution)/shard_map/all_to_all | solution.py:604
  57.3 10.0 %shard_map.133 = (bf16[64,32,128]{2,1,0:T(8,128)(2,1)}, bf16[128,8,128]{2,1,0:T(8,128)(2,1)}) custom-call(bf16[512,512]{1,0:T(8,128)(2,1)} %get-tuple-element.18.taps_ref, bf16[128,512]{1,0:T(8,128)(2,1)} %get-tuple-element.25.last_ref, f32[1,128]{1,0:T(1,128)} %broadcast_in_dim_tile.7.bias_ref, f32[1,256]{1,0:T(1,128)} %weight_ref.3, ...), custom_call_target="tpu_custom_call" | custom-call | flops 8589934592 | bytes 1048576 | tf_op jit(solution)/shard_map/pallas_call | solution.py:593
  67.3 4.1 %all-to-all-done.1.refs_0_ = bf16[128,16,128]{2,1,0:T(8,128)(2,1)S(1)} async-done(((bf16[128,16,128]{2,1,0:T(8,128)(2,1)}), bf16[128,16,128]{2,1,0:T(8,128)(2,1)S(1)}, u32[]{:S(2)}, u32[]{:S(2)}) %all-to-all-start.1) | async-done | bytes 524320 | tf_op jit(solution)/shard_map/all_to_all | solution.py:604
  71.4 0.9 copy-done
  72.3 0.2 shard_map.134
  72.5 22.3 %all_to_all.15.arrived_ref = bf16[128,24,128]{2,1,0:T(8,128)(2,1)S(1)} all-to-all(bf16[128,24,128]{2,1,0:T(8,128)(2,1)S(1)} %shard_map.134), channel_id=1, replica_groups=mesh['gx'=16,'gy'=8] {'gx','gy'}, dimensions={0} | all-to-all | bytes 1572864 | tf_op jit(solution)/shard_map/all_to_all | solution.py:604
  94.8 1.7 %shard_map.135 = (f32[4096,64]{1,0:T(8,128)}, f32[16,64]{1,0:T(8,128)}) custom-call(bf16[128,24,128]{2,1,0:T(8,128)(2,1)S(1)} %all_to_all.15.arrived_ref), custom_call_target="tpu_custom_call" | custom-call | flops 268435456 | bytes 1048576 | tf_op jit(solution)/shard_map/pallas_call | solution.py:600
  (5 shorter events, 0.0 us)
Async XLA Ops:
  4.3 11.7 %copy-start.3 = (f32[64]{0:T(128)S(1)}, f32[64]{0:T(128)}, u32[]{:S(2)}) copy-start(f32[64]{0:T(128)} %param.13) | copy-start | bytes 772
  4.4 12.4 %copy-start.4 = (f32[64]{0:T(128)S(1)}, f32[64]{0:T(128)}, u32[]{:S(2)}) copy-start(f32[64]{0:T(128)} %param.15) | copy-start | bytes 772
  4.4 13.0 %copy-start.2 = (bf16[3,3,3,8,64]{4,3,2,1,0:T(8,128)(2,1)S(1)}, bf16[3,3,3,8,64]{4,3,2,1,0:T(8,128)(2,1)}, u32[]{:S(2)}) copy-start(bf16[3,3,3,8,64]{4,3,2,1,0:T(8,128)(2,1)} %param.12) | copy-start | bytes 82948
  4.4 33.8 %all-to-all-start = ((bf16[128,40,128]{2,1,0:T(8,128)(2,1)}), bf16[128,40,128]{2,1,0:T(8,128)(2,1)S(1)}, u32[]{:S(2)}, u32[]{:S(2)}) async-start(bf16[128,40,128]{2,1,0:T(8,128)(2,1)} %bitcast.10), calls=%async_computation | async-start | bytes 2621440 | tf_op jit(solution)/shard_map/all_to_all | solution.py:604
  38.2 1.1 %copy-start.1 = (bf16[128,40,128]{2,1,0:T(8,128)(2,1)}, bf16[128,40,128]{2,1,0:T(8,128)(2,1)S(1)}, u32[]{:S(2)}) copy-start(bf16[128,40,128]{2,1,0:T(8,128)(2,1)S(1)} %all-to-all-done.arrived_far) | copy-start | bytes 3932164
  53.4 18.0 %all-to-all-start.1 = ((bf16[128,16,128]{2,1,0:T(8,128)(2,1)}), bf16[128,16,128]{2,1,0:T(8,128)(2,1)S(1)}, u32[]{:S(2)}, u32[]{:S(2)}) async-start(bf16[128,16,128]{2,1,0:T(8,128)(2,1)} %get-tuple-element.29), calls=%async_computation.1 | async-start | bytes 1048576 | tf_op jit(solution)/shard_map/all_to_all | solution.py:604
  71.4 1.0 copy-start
